TPU v7x, 32 devices: a whole 2x2x4 slice. The times are simulated.
32 devices in a mesh: row: 8 (over y, x, core), col: 4 (over z).
Axes of the slice: x: 2, y: 2, z: 4, core: 2. Of those that a mesh axis runs over, the one named last changes fastest.
Arguments:
- inverse_tiles: float32 [512, 512], P('row', 'col'), may hold values from -0.375 to 0.375
- factor_panels: float32 [3, 512, 256], P(None, 'row', 'col'), may hold values from -6 to 6
- block_rows: int32 [3, 8], replicated, may hold values from 0 to 15, as said below
- couplings: float32 [2, 512, 512], replicated, may hold values from -0.25 to 0.25
Outputs:
- new_columns: float32 [3, 512, 512], P(None, ('row', 'col'))
Inputs may be any that keep to these rules, and one draw needn't show every extreme that they name: `block_rows`: each row lists 8 different row blocks in no particular order; in each row, all 4 blocks q * 4 to q * 4 + 3 of some q are listed.
All inputs are finite; a program needn't handle non-finite values.
Results may differ from a plain program's by a relative error of at most 0.0001.
Values sent between devices are 32-bit elements; how exact they have to be, the bound alone decides.
No kernel may reach another device: no remote copies, remote signals or barrier semaphores. Data moves between devices by JAX's collectives and lax.ppermute only.
A program may use at most 64 MiB of HBM per device.

v0:
```python
import jax
import jax.numpy as jnp
from jax import lax
from jax.sharding import PartitionSpec as P


def on_device(inverse_tiles, factor_panels, block_rows, couplings):
    tile_rows, tile_cols = inverse_tiles.shape
    piece_rows = factor_panels.shape[1]
    listed = block_rows.shape[1]
    col_count = lax.axis_size("col")
    block_size = factor_panels.shape[2] * col_count // listed
    local_blocks = tile_cols // block_size
    my_column = lax.axis_index("col")
    offset = my_column * local_blocks
    targets = offset + jnp.arange(local_blocks, dtype=jnp.int32)
    results = []
    previous = None
    for section in range(factor_panels.shape[0]):
        section_rows = block_rows[section]
        gathered = lax.all_gather(factor_panels[section], "col", axis=1, tiled=True)
        onehot = (section_rows[:, None] == targets[None, :]).astype(jnp.float32)
        picked = jnp.einsum(
            "wpr,pq->wqr",
            gathered.reshape(piece_rows, listed, block_size),
            onehot,
            precision=lax.Precision.HIGHEST,
        ).reshape(piece_rows, tile_cols)
        partial_value = lax.dot_general(
            inverse_tiles,
            lax.all_gather(picked, "row", axis=0, tiled=True),
            (((1,), (1,)), ((), ())),
            precision=lax.Precision.HIGHEST,
            preferred_element_type=jnp.float32,
        )
        summed = lax.psum_scatter(partial_value, "col", scatter_dimension=0, tiled=True)
        if previous is not None:
            summed = summed + jnp.dot(
                previous,
                couplings[section - 1],
                precision=lax.Precision.HIGHEST,
                preferred_element_type=jnp.float32,
            )
        previous = -summed
        results.append(previous)
    return jnp.stack(results)


def solution(mesh):
    return jax.shard_map(
        on_device,
        mesh=mesh,
        in_specs=(P("row", "col"), P(None, "row", "col"), P(), P()),
        out_specs=P(None, ("row", "col"), None),
        check_vma=False,
    )
```

profile of v0, /device:TPU:0, one launch (start us, length us, event | category | flops | bytes accessed | tf_op | source)
XLA Modules:
  0.0 111.6 jit_solution(15987718816973304762)
XLA Ops:
  6.5 0.0 copy-start
  6.5 0.0 reduce-scatter.4.cloned.1.call-start
  6.5 0.8 fusion.23
  7.3 0.1 copy.26
  7.4 15.1 %all-gather = f32[1,64,256]{1,2,0:T(8,128)S(1)} all-gather(f32[1,64,64]{1,2,0:T(8,128)S(1)} %copy.26), channel_id=2, replica_groups=mesh['row'=8,'col'=4] {'col'}, dimensions={2}, use_global_device_ids=true | all-gather | bytes 81920 | tf_op jit(solution)/shard_map/all_gather | solution.py:21
  22.5 0.8 slice_bitcast_fusion.2
  23.3 0.3 convolution_bitcast_fusion.5
  23.6 0.0 copy-start.1
  23.6 0.1 copy.17
  23.7 9.4 %all_gather.19 = f32[512,128]{1,0:T(8,128)S(1)} all-gather(f32[64,128]{1,0:T(8,128)S(1)} %copy.17), channel_id=1, replica_groups=mesh['row'=8,'col'=4] {'row'}, dimensions={0}, use_global_device_ids=true | all-gather | bytes 294912 | tf_op jit(solution)/shard_map/all_gather | solution.py:31
  33.1 0.0 copy-done
  33.1 1.1 convolution_bitcast_fusion.2
  34.2 0.0 reduce-scatter.4.cloned.1.call-update
  34.2 0.0 reduce-scatter.6.cloned.1.call-start
  34.3 0.1 copy.27
  34.3 13.5 %all-gather.1 = f32[1,64,256]{1,2,0:T(8,128)S(1)} all-gather(f32[1,64,64]{1,2,0:T(8,128)S(1)} %copy.27), channel_id=3, replica_groups=mesh['row'=8,'col'=4] {'col'}, dimensions={2}, use_global_device_ids=true | all-gather | bytes 81920 | tf_op jit(solution)/shard_map/all_gather | solution.py:21
  47.9 0.3 convolution_bitcast_fusion.4
  48.2 0.1 copy.21
  48.2 9.3 %all_gather.21 = f32[512,128]{1,0:T(8,128)S(1)} all-gather(f32[64,128]{1,0:T(8,128)S(1)} %copy.21), channel_id=1, replica_groups=mesh['row'=8,'col'=4] {'row'}, dimensions={0}, use_global_device_ids=true | all-gather | bytes 294912 | tf_op jit(solution)/shard_map/all_gather | solution.py:31
  57.5 1.1 convolution_bitcast_fusion.1
  58.6 0.0 reduce-scatter.6.cloned.1.call-update
  58.6 0.0 reduce-scatter.8.cloned.1.call-start
  58.6 0.1 copy.28
  58.7 13.7 %all-gather.2 = f32[1,64,256]{1,2,0:T(8,128)S(1)} all-gather(f32[1,64,64]{1,2,0:T(8,128)S(1)} %copy.28), channel_id=4, replica_groups=mesh['row'=8,'col'=4] {'col'}, dimensions={2}, use_global_device_ids=true | all-gather | bytes 81920 | tf_op jit(solution)/shard_map/all_gather | solution.py:21
  72.4 0.3 convolution_bitcast_fusion.3
  72.7 0.1 copy.25
  72.8 8.7 %all_gather.23 = f32[512,128]{1,0:T(8,128)S(1)} all-gather(f32[64,128]{1,0:T(8,128)S(1)} %copy.25), channel_id=1, replica_groups=mesh['row'=8,'col'=4] {'row'}, dimensions={0}, use_global_device_ids=true | all-gather | bytes 294912 | tf_op jit(solution)/shard_map/all_gather | solution.py:31
  81.5 1.1 convolution_bitcast_fusion
  82.6 0.0 reduce-scatter.8.cloned.1.call-update
  82.6 0.0 reduce-scatter.4.cloned.1.call-done
  82.7 0.8 negate_bitcast_fusion
  83.4 0.0 reduce-scatter.6.cloned.1.call-done
  83.4 0.0 copy-done.1
  83.4 1.4 %fusion.2 = f32[16,512]{1,0:T(8,128)S(1)} fusion(f32[16,512]{1,0:T(8,128)} %reduce-scatter.6.cloned.1.call-done, f32[2,512,512]{2,1,0:T(8,128)S(1)} %copy-done.1, f32[16,512]{1,0:T(8,128)} %reduce-scatter.4.cloned.1.call-done), kind=kOutput, calls=%fused_computation.10 | convolution fusion | flops 50356224 | bytes 1146880 | tf_op jit(solution)/shard_map/dot_general | solution.py:38
  84.8 18.2 %reduce-scatter.8.cloned.1.call-done = f32[16,512]{1,0:T(8,128)} async-done(((f32[64,512]{1,0:T(8,128)}), f32[16,512]{1,0:T(8,128)}) %reduce-scatter.8.cloned.1.call-update) | async-done | bytes 32784 | tf_op jit(solution)/shard_map/reduce_scatter | solution.py:36
  103.0 1.4 %fusion.1 = f32[1,16,512]{2,1,0:T(8,128)S(1)} fusion(f32[16,512]{1,0:T(8,128)} %reduce-scatter.8.cloned.1.call-done, f32[16,512]{1,0:T(8,128)S(1)} %fusion.2, f32[2,512,512]{2,1,0:T(8,128)S(1)} %copy-done.1), kind=kOutput, calls=%fused_computation.8 | convolution fusion | flops 50348032 | bytes 1146880 | tf_op jit(solution)/shard_map/dot_general | solution.py:38
  104.4 0.6 pad_maximum_fusion
  (4 shorter events, 0.0 us)
Async XLA Ops:
  6.5 26.6 %copy-start = (f32[64,128]{1,0:T(8,128)S(1)}, f32[64,128]{1,0:T(8,128)}, u32[]{:S(2)}) copy-start(f32[64,128]{1,0:T(8,128)} %param.4) | copy-start | bytes 98308
  6.5 76.1 %reduce-scatter.4.cloned.1.call-start = ((), (), s32[]{:S(2)}) async-start(), calls=%async_computation.3 | async-start | bytes 163840 | tf_op jit(solution)/shard_map/reduce_scatter | solution.py:36
  23.6 59.9 %copy-start.1 = (f32[2,512,512]{2,1,0:T(8,128)S(1)}, f32[2,512,512]{2,1,0:T(8,128)}, u32[]{:S(2)}) copy-start(f32[2,512,512]{2,1,0:T(8,128)} %param.7) | copy-start | bytes 6291460
  34.2 49.2 %reduce-scatter.6.cloned.1.call-start = ((), (), s32[]{:S(2)}) async-start(), calls=%async_computation.4 | async-start | bytes 163840 | tf_op jit(solution)/shard_map/reduce_scatter | solution.py:36
  58.6 44.4 %reduce-scatter.8.cloned.1.call-start = ((), (), s32[]{:S(2)}) async-start(), calls=%async_computation.5 | async-start | bytes 163840 | tf_op jit(solution)/shard_map/reduce_scatter | solution.py:36
Sparse Core Ops, SparseCore 0:
  34.3 19.9 reduce-scatter.3
  58.7 20.2 reduce-scatter.5
  82.8 20.2 reduce-scatter.7
where the time goes:
time: 112 us
  blocking collectives  69.8 us (62%)
  waiting for transfers between devices  18.3 us (16%)
  between operations  13.2 us (12%)
  matrix products  6.76 us (6%)
  local copies, waits for them, and re-layouts  2.04 us (2%)
  other arithmetic  1.41 us (1%)
    all_gather x3, blocking collectives, on_device(): gathered = lax.all_gather(factor_panels[section], 'col', axis=1, tiled=True)  42.3 us
    all_gather x3, blocking collectives, on_device(): lax.all_gather(picked, 'row', axis=0, tiled=True)  27.5 us
    reduce_scatter x3, waiting for transfers between devices, on_device(): lax.psum_scatter(partial_value, 'col', scatter_dimension=0, tiled=True)  18.2 us
    dot_general x3, matrix products, on_device(): lax.dot_general(inverse_tiles, lax.all_gather(picked, 'row', axis=0, tile...  3.21 us
    dot_general x2, matrix products, on_device(): jnp.dot(previous, couplings[section - 1], precision=lax.Precision.HIGHEST...  2.76 us
  transfers between devices with their start and end apart: 3, of which 1 were waited for; matrix products, arithmetic and copies ran while one was open for 5% of the time, Pallas kernels for 0%

commit v1 on v0

--- a/solution.py
+++ b/solution.py
@@ -1,11 +1,23 @@
+import functools
+
 import jax
 import jax.numpy as jnp
 from jax import lax
+from jax.experimental import pallas as pl
+from jax.experimental.pallas import tpu as pltpu
 from jax.sharding import PartitionSpec as P
 
 
-def on_device(inverse_tiles, factor_panels, block_rows, couplings):
-    tile_rows, tile_cols = inverse_tiles.shape
+LANES = 128
+CORES = 2
+REPLICA_BYTES = 4 << 20
+KERNEL_BYTES = 12 << 20
+VMEM = pl.BlockSpec(memory_space=pltpu.VMEM)
+SMEM = pl.BlockSpec(memory_space=pltpu.SMEM)
+
+
+def streamed(inverse_tiles, factor_panels, block_rows, couplings):
+    _, tile_cols = inverse_tiles.shape
     piece_rows = factor_panels.shape[1]
     listed = block_rows.shape[1]
     col_count = lax.axis_size("col")
@@ -46,6 +58,185 @@
     return jnp.stack(results)
 
 
+def call(kernel, out_shape, specs, scratch=()):
+    run = pl.pallas_call(
+        kernel,
+        out_shape=out_shape,
+        in_specs=specs,
+        out_specs=jax.tree.map(lambda _: VMEM, out_shape),
+        scratch_shapes=scratch,
+        compiler_params=pltpu.CompilerParams(vmem_limit_bytes=KERNEL_BYTES),
+    )
+    return run
+
+
+def split(value):
+    high = value.astype(jnp.bfloat16)
+    return high, (value - high.astype(jnp.float32)).astype(jnp.bfloat16)
+
+
+def swap(value, axis, distance):
+    count = lax.axis_size(axis)
+    return lax.ppermute(value, axis, [(i, i ^ distance) for i in range(count)])
+
+
+def pack_kernel(rows, fold, tile_ref, panel_ref, *outs):
+    column = lax.axis_index("col")
+    high = panel_ref.shape[1] // fold
+    for section in range(panel_ref.shape[0]):
+        dense = jnp.concatenate(
+            [panel_ref[section, i * high : (i + 1) * high, :] for i in range(fold)], axis=1
+        )
+        for out in outs:
+            out[section * high : (section + 1) * high, :] = dense
+    for away, out in enumerate(outs):
+        start = pl.multiple_of((column ^ away) * rows, rows)
+        out[panel_ref.shape[0] * high :, :] = tile_ref[pl.ds(start, rows), :]
+
+
+def join_kernel(*refs):
+    *parts, inverse, line = refs
+    depth = line.shape[0] // len(parts)
+    for away, part in enumerate(parts):
+        inverse[:, away * LANES : (away + 1) * LANES] = part[depth:, :]
+        line[away * depth : (away + 1) * depth, :] = part[:depth, :]
+
+
+def couplings_kernel(couplings, high_ref, low_ref):
+    high, low = split(couplings[...])
+    high_ref[...] = high
+    low_ref[...] = low
+
+
+def place_kernel(fold, blocks_here, listed_here, block_size, block_rows, own_ref, other_ref, high_ref, low_ref):
+    column = lax.axis_index("col")
+    core = lax.rem(lax.axis_index("row"), CORES)
+    sections = block_rows.shape[0]
+    cols = high_ref.shape[0] // LANES
+    width = listed_here * block_size
+    depth = own_ref.shape[0] // cols // sections
+    high_ref[...] = jnp.zeros_like(high_ref)
+    low_ref[...] = jnp.zeros_like(low_ref)
+    for section in range(sections):
+        for first in range(0, cols, fold):
+            pieces = []
+            for e in range(CORES):
+                parts = []
+                for away in range(first, first + fold):
+                    at = (away * sections + section) * depth
+                    own, other = own_ref[at : at + depth, :], other_ref[at : at + depth, :]
+                    parts.append(jnp.where(core == e, own, other))
+                for i in range(fold):
+                    pieces.append(
+                        jnp.concatenate([part[:, i * width : (i + 1) * width] for part in parts], axis=1)
+                    )
+            high, low = split(jnp.concatenate(pieces, axis=0).T)
+            for place in range(fold):
+                for block in range(listed_here):
+                    row = block_rows[section, (column ^ (first + place)) * listed_here + block]
+                    tile = (row // blocks_here) ^ column
+                    start = tile * LANES + (row % blocks_here) * block_size
+                    target = pl.ds(pl.multiple_of(start, block_size), block_size)
+                    at = place * width + block * block_size
+                    lanes = slice(section * LANES, (section + 1) * LANES)
+                    high_ref[target, lanes] = high[at : at + block_size]
+                    low_ref[target, lanes] = low[at : at + block_size]
+
+
+def product(stacked, high, low):
+    half = stacked.shape[0] // 2
+    first = jnp.dot(stacked, high, preferred_element_type=jnp.float32)
+    second = jnp.dot(stacked, low, preferred_element_type=jnp.float32)
+    total = first + second
+    return total[:half] + total[half:]
+
+
+def multiply_kernel(*refs):
+    half = (len(refs) - 2) // 2
+    inverses, (high_ref, low_ref), outs = refs[:half], refs[half : half + 2], refs[half + 2 :]
+    rows = inverses[0].shape[0]
+    stacked = jnp.concatenate(split(jnp.concatenate([ref[...] for ref in inverses], axis=0)), axis=0)
+    total = product(stacked, high_ref[...], low_ref[...])
+    for chip, out in enumerate(outs):
+        for section in range(total.shape[1] // LANES):
+            out[section * rows : (section + 1) * rows, :] = total[
+                chip * rows : (chip + 1) * rows, section * LANES : (section + 1) * LANES
+            ]
+
+
+def finish_kernel(*refs):
+    *parts, high_ref, low_ref, out = refs
+    sections, rows, _ = out.shape
+    chip = lax.div(lax.axis_index("row"), CORES)
+    previous = None
+    for section in range(sections):
+        tiles = [part[section * rows : (section + 1) * rows, :] for part in parts]
+        step = 1
+        while step < len(tiles):
+            tiles = [
+                jnp.where((chip & step) != 0, tiles[i ^ step], tile) for i, tile in enumerate(tiles)
+            ]
+            step *= 2
+        value = jnp.concatenate(tiles, axis=1)
+        if previous is not None:
+            stacked = jnp.concatenate(split(previous), axis=0)
+            value = value + product(stacked, high_ref[section - 1], low_ref[section - 1])
+        previous = -value
+        out[section] = previous
+
+
+def gathered(inverse_tiles, factor_panels, block_rows, couplings):
+    f32 = jnp.float32
+    sections, piece_rows, width = factor_panels.shape
+    count, cols = lax.axis_size("row"), lax.axis_size("col")
+    listed = block_rows.shape[1]
+    block_size = width * cols // listed
+    fold = LANES // width
+    rows = inverse_tiles.shape[0] // cols
+    order = inverse_tiles.shape[1] * cols
+    depth = sections * piece_rows // fold
+
+    bf16 = jnp.bfloat16
+    chips = range(0, count, CORES)
+
+    packed = call(
+        functools.partial(pack_kernel, rows, fold),
+        [jax.ShapeDtypeStruct((depth + rows, LANES), f32)] * cols,
+        [VMEM, VMEM],
+    )(inverse_tiles, factor_panels)
+    arrived = [packed[0]] + [swap(packed[away], "col", away) for away in range(1, cols)]
+    inverse, line = call(
+        join_kernel,
+        [jax.ShapeDtypeStruct((rows, order), f32), jax.ShapeDtypeStruct((cols * depth, LANES), f32)],
+        [VMEM] * cols,
+    )(*arrived)
+    inverses = [inverse] + [swap(inverse, "row", chip) for chip in chips[1:]]
+    placed = call(
+        functools.partial(place_kernel, fold, LANES // block_size, listed // cols, block_size),
+        [jax.ShapeDtypeStruct((order, sections * LANES), bf16)] * 2,
+        [SMEM, VMEM, VMEM],
+    )(block_rows, line, swap(line, "row", 1))
+    products = call(
+        multiply_kernel, [jax.ShapeDtypeStruct((sections * rows, LANES), f32)] * len(chips), [VMEM] * (len(chips) + 2)
+    )(*inverses, *placed)
+    returned = [products[0]] + [swap(products[i], "row", chip) for i, chip in enumerate(chips) if chip]
+    halves = call(couplings_kernel, [jax.ShapeDtypeStruct(couplings.shape, bf16)] * 2, [VMEM])(couplings)
+    return call(
+        finish_kernel, jax.ShapeDtypeStruct((sections, rows, piece_rows * count), f32), [VMEM] * (len(chips) + 2)
+    )(*returned, *halves)
+
+
+def on_device(inverse_tiles, factor_panels, block_rows, couplings):
+    sections, piece_rows, width = factor_panels.shape
+    count, cols = lax.axis_size("row"), lax.axis_size("col")
+    powers = all(n & (n - 1) == 0 for n in (count, cols))
+    fits = sections * piece_rows * width * count * cols * 4 <= REPLICA_BYTES
+    lanes = inverse_tiles.shape[1] == LANES == CORES * piece_rows and LANES % width == 0
+    if powers and fits and lanes and count % CORES == 0 == cols % (LANES // width):
+        return gathered(inverse_tiles, factor_panels, block_rows, couplings)
+    return streamed(inverse_tiles, factor_panels, block_rows, couplings)
+
+
 def solution(mesh):
     return jax.shard_map(
         on_device,

time: 112 us -> 29 us (0.26)
  blocking collectives: 69.8 us -> 0 us
  between operations: 13.2 us -> 0.07 us
  starting transfers between devices: 0.09 us -> 12.9 us
  waiting for transfers between devices: 18.3 us -> 9.14 us
  matrix products: 6.76 us -> 0 us
  Pallas kernels: 0 us -> 2.76 us
  local copies, waits for them, and re-layouts: 2.04 us -> 3.92 us
  other arithmetic: 1.41 us -> 0 us
    all_gather x6 -> x0, blocking collectives: 69.8 us -> none  [the longest x3 42.3 us: on_device(): gathered = lax.all_gather(factor_panels[section], 'col', axis=1, tiled=True)]
    reduce_scatter x3 -> x0, waiting for transfers between devices: 18.2 us -> none  [on_device(): lax.psum_scatter(partial_value, 'col', scatter_dimension=0, tiled=True)]
    ppermute x0 -> x10, starting transfers between devices: none -> 12.9 us  [swap(): return lax.ppermute(value, axis, [(i, i ^ distance) for i in range(count)])]
    ppermute x0 -> x10, waiting for transfers between devices: none -> 9.14 us  [swap(): return lax.ppermute(value, axis, [(i, i ^ distance) for i in range(count)])]
    dot_general x8 -> x0, matrix products: 6.76 us -> none  [the longest x3 3.21 us: on_device(): lax.dot_general(inverse_tiles, lax.all_gather(picked, 'row', axis=0, tile...]
    unnamed x7 -> x8, local copies, waits for them, and re-layouts: 0.23 us -> 3.92 us
    pallas_call x0 -> x6, Pallas kernels: none -> 2.76 us  [the longest x1 1.17 us: gathered(): call(finish_kernel, jax.ShapeDtypeStruct((sections, rows, piece_rows * co...]
    another operation x2 -> x0, other arithmetic: 1.41 us -> none  [on_device(): return jnp.stack(results)]
  transfers between devices with their start and end apart: 3 -> 10, of which waited for: 1 -> 5; matrix products, arithmetic and copies ran while one was open for 5% -> 0% of each run, Pallas kernels for 0% -> 4%
where the time goes in v1:
time: 29 us; the launch traced here: 28.8 us
  starting transfers between devices  12.9 us (44%)
  waiting for transfers between devices  9.14 us (32%)
  local copies, waits for them, and re-layouts  3.92 us (14%)
  Pallas kernels  2.76 us (10%)
    ppermute x10, starting transfers between devices, swap(): return lax.ppermute(value, axis, [(i, i ^ distance) for i in range(count)])  12.9 us
    ppermute x10, waiting for transfers between devices, swap(): return lax.ppermute(value, axis, [(i, i ^ distance) for i in range(count)])  9.14 us
    unnamed x8, local copies, waits for them, and re-layouts  3.92 us
    pallas_call x1, Pallas kernels, gathered(): call(finish_kernel, jax.ShapeDtypeStruct((sections, rows, piece_rows * co...  1.17 us
    pallas_call x1, Pallas kernels, gathered(): call(functools.partial(place_kernel, fold, LANES // block_size, listed //...  0.9 us
  transfers between devices with their start and end apart: 10, of which 5 were waited for; matrix products, arithmetic and copies ran while one was open for 0% of the time, Pallas kernels for 4%

profile of v1, /device:TPU:0, one launch (start us, length us, event | category | flops | bytes accessed | tf_op | source)
XLA Modules:
  0.0 28.8 jit_solution(12912666714983658957)
XLA Ops:
  0.0 0.0 copy-start.1
  0.0 0.9 %copy-done.1 = f32[3,64,64]{2,1,0:T(8,128)S(1)} copy-done((f32[3,64,64]{2,1,0:T(8,128)S(1)}, f32[3,64,64]{2,1,0:T(8,128)}, u32[]{:S(2)}) %copy-start.1) | copy-done | bytes 49176
  0.9 0.0 copy-start.2
  0.9 0.8 %copy-done.2 = f32[64,128]{1,0:T(8,128)S(1)} copy-done((f32[64,128]{1,0:T(8,128)S(1)}, f32[64,128]{1,0:T(8,128)}, u32[]{:S(2)}) %copy-start.2) | copy-done | bytes 32792
  1.7 0.1 shard_map.46
  1.7 3.1 %collective-permute-start = (f32[112,128]{1,0:T(8,128)S(1)}, f32[112,128]{1,0:T(8,128)S(1)}, u32[]{:S(2)}, u32[]{:S(2)}) collective-permute-start(f32[112,128]{1,0:T(8,128)S(1)} %get-tuple-element.20), channel_id=1, source_target_pairs={{0,1},{1,0},{2,3},{3,2},{4,5},{5,4},{6,7},{7,6},{8,9},{9,8},{10,11... | collective-permute-start | bytes 172040 | tf_op jit(solution)/shard_map/ppermute | solution.py:80
  4.9 2.6 %collective-permute-start.1 = (f32[112,128]{1,0:T(8,128)S(1)}, f32[112,128]{1,0:T(8,128)S(1)}, u32[]{:S(2)}, u32[]{:S(2)}) collective-permute-start(f32[112,128]{1,0:T(8,128)S(1)} %get-tuple-element.21), channel_id=1, source_target_pairs={{0,2},{1,3},{2,0},{3,1},{4,6},{5,7},{6,4},{7,5},{8,10},{9,11},{10,... | collective-permute-start | bytes 172040 | tf_op jit(solution)/shard_map/ppermute | solution.py:80
  7.4 0.0 collective-permute-start.2
  7.4 0.0 collective-permute-done.refs_1_
  7.5 3.6 %collective-permute-done.1.refs_2_ = f32[112,128]{1,0:T(8,128)S(1)} collective-permute-done((f32[112,128]{1,0:T(8,128)S(1)}, f32[112,128]{1,0:T(8,128)S(1)}, u32[]{:S(2)}, u32[]{:S(2)}) %collective-permute-start.1) | collective-permute-done | bytes 57376 | tf_op jit(solution)/shard_map/ppermute | solution.py:80
  11.0 2.4 %collective-permute-done.2.refs_3_ = f32[112,128]{1,0:T(8,128)S(1)} collective-permute-done((f32[112,128]{1,0:T(8,128)S(1)}, f32[112,128]{1,0:T(8,128)S(1)}, u32[]{:S(2)}, u32[]{:S(2)}) %collective-permute-start.2) | collective-permute-done | bytes 57376 | tf_op jit(solution)/shard_map/ppermute | solution.py:80
  13.4 0.1 collective-permute-start.6
  13.5 2.5 %collective-permute-start.5 = (f32[16,512]{1,0:T(8,128)S(1)}, f32[16,512]{1,0:T(8,128)S(1)}, u32[]{:S(2)}, u32[]{:S(2)}) collective-permute-start(f32[16,512]{1,0:T(8,128)S(1)} %get-tuple-element.23.refs_0_), channel_id=1, source_target_pairs={{0,24},{4,28},{8,16},{12,20},{16,8},{20,12},{24,0},{28,4},{1,25},{... | collective-permute-start | bytes 98312 | tf_op jit(solution)/shard_map/ppermute | solution.py:80
  16.0 0.5 %collective-permute-start.4 = (f32[16,512]{1,0:T(8,128)S(1)}, f32[16,512]{1,0:T(8,128)S(1)}, u32[]{:S(2)}, u32[]{:S(2)}) collective-permute-start(f32[16,512]{1,0:T(8,128)S(1)} %get-tuple-element.23.refs_0_), channel_id=1, source_target_pairs={{0,16},{4,20},{8,24},{12,28},{16,0},{20,4},{24,8},{28,12},{1,17},{... | collective-permute-start | bytes 98312 | tf_op jit(solution)/shard_map/ppermute | solution.py:80
  16.5 0.5 %collective-permute-start.3 = (f32[16,512]{1,0:T(8,128)S(1)}, f32[16,512]{1,0:T(8,128)S(1)}, u32[]{:S(2)}, u32[]{:S(2)}) collective-permute-start(f32[16,512]{1,0:T(8,128)S(1)} %get-tuple-element.23.refs_0_), channel_id=1, source_target_pairs={{0,8},{4,12},{8,0},{12,4},{16,24},{20,28},{24,16},{28,20},{1,9},{5... | collective-permute-start | bytes 98312 | tf_op jit(solution)/shard_map/ppermute | solution.py:80
  17.1 0.0 collective-permute-done.6.other_ref
  17.1 0.0 copy-start.3
  17.1 0.7 %copy-done.3 = s32[3,8]{1,0:T(4,128)S(1)} copy-done((s32[3,8]{1,0:T(4,128)S(1)}, s32[3,8]{1,0:T(4,128)}, u32[]{:S(2)}) %copy-start.3) | copy-done | bytes 120
  17.8 0.9 %shard_map.48 = (bf16[512,384]{1,0:T(8,128)(2,1)S(1)}, bf16[512,384]{1,0:T(8,128)(2,1)S(1)}) custom-call(s32[3,8]{1,0:T(4,128)S(1)} %copy-done.3, f32[384,128]{1,0:T(8,128)S(1)} %get-tuple-element.24.own_ref, f32[384,128]{1,0:T(8,128)S(1)} %collective-permute-done.6.other_ref), custom_call_target="tpu_custom_call" | custom-call | tf_op jit(solution)/shard_map/pallas_call | solution.py:214
  18.7 0.0 collective-permute-done.5.refs_3_
  18.7 1.3 %collective-permute-done.4.refs_2_ = f32[16,512]{1,0:T(8,128)S(1)} collective-permute-done((f32[16,512]{1,0:T(8,128)S(1)}, f32[16,512]{1,0:T(8,128)S(1)}, u32[]{:S(2)}, u32[]{:S(2)}) %collective-permute-start.4) | collective-permute-done | bytes 32800 | tf_op jit(solution)/shard_map/ppermute | solution.py:80
  19.9 0.5 %collective-permute-done.3.refs_1_ = f32[16,512]{1,0:T(8,128)S(1)} collective-permute-done((f32[16,512]{1,0:T(8,128)S(1)}, f32[16,512]{1,0:T(8,128)S(1)}, u32[]{:S(2)}, u32[]{:S(2)}) %collective-permute-start.3) | collective-permute-done | bytes 32800 | tf_op jit(solution)/shard_map/ppermute | solution.py:80
  20.5 0.3 %shard_map.49 = (f32[48,128]{1,0:T(8,128)S(1)}, f32[48,128]{1,0:T(8,128)S(1)}, f32[48,128]{1,0:T(8,128)S(1)}, f32[48,128]{1,0:T(8,128)S(1)}) custom-call(f32[16,512]{1,0:T(8,128)S(1)} %get-tuple-element.23.refs_0_, f32[16,512]{1,0:T(8,128)S(1)} %collective-permute-done.3.refs_1_, f32[16,512]{1,0:T(8,128)S(1)} %collective-permute-done.4.refs_2_, ...), custom_call_target="tpu_custom_call" | custom-call | tf_op jit(solution)/shard_map/pallas_call | solution.py:219
  20.8 0.6 %collective-permute-start.7 = (f32[48,128]{1,0:T(8,128)S(1)}, f32[48,128]{1,0:T(8,128)S(1)}, u32[]{:S(2)}, u32[]{:S(2)}) collective-permute-start(f32[48,128]{1,0:T(8,128)S(1)} %get-tuple-element.28), channel_id=1, source_target_pairs={{0,8},{4,12},{8,0},{12,4},{16,24},{20,28},{24,16},{28,20},{1,9},{5... | collective-permute-start | bytes 73736 | tf_op jit(solution)/shard_map/ppermute | solution.py:80
  21.4 1.5 %collective-permute-start.8 = (f32[48,128]{1,0:T(8,128)S(1)}, f32[48,128]{1,0:T(8,128)S(1)}, u32[]{:S(2)}, u32[]{:S(2)}) collective-permute-start(f32[48,128]{1,0:T(8,128)S(1)} %get-tuple-element.29), channel_id=1, source_target_pairs={{0,16},{4,20},{8,24},{12,28},{16,0},{20,4},{24,8},{28,12},{1,17},{... | collective-permute-start | bytes 73736 | tf_op jit(solution)/shard_map/ppermute | solution.py:80
  22.9 1.4 %collective-permute-start.9 = (f32[48,128]{1,0:T(8,128)S(1)}, f32[48,128]{1,0:T(8,128)S(1)}, u32[]{:S(2)}, u32[]{:S(2)}) collective-permute-start(f32[48,128]{1,0:T(8,128)S(1)} %get-tuple-element.30), channel_id=1, source_target_pairs={{0,24},{4,28},{8,16},{12,20},{16,8},{20,12},{24,0},{28,4},{1,25},{... | collective-permute-start | bytes 73736 | tf_op jit(solution)/shard_map/ppermute | solution.py:80
  24.3 0.0 copy-start
  24.3 1.6 %copy-done = f32[2,512,512]{2,1,0:T(8,128)S(1)} copy-done((f32[2,512,512]{2,1,0:T(8,128)S(1)}, f32[2,512,512]{2,1,0:T(8,128)}, u32[]{:S(2)}) %copy-start) | copy-done | bytes 2097176
  25.9 0.3 %shard_map.50 = (bf16[2,512,512]{2,1,0:T(8,128)(2,1)S(1)}, bf16[2,512,512]{2,1,0:T(8,128)(2,1)S(1)}) custom-call(f32[2,512,512]{2,1,0:T(8,128)S(1)} %copy-done), custom_call_target="tpu_custom_call" | custom-call | tf_op jit(solution)/shard_map/pallas_call | solution.py:223
  26.2 0.0 collective-permute-done.7.refs_1_
  26.2 0.0 collective-permute-done.8.refs_2_
  26.2 1.4 %collective-permute-done.9.refs_3_ = f32[48,128]{1,0:T(8,128)S(1)} collective-permute-done((f32[48,128]{1,0:T(8,128)S(1)}, f32[48,128]{1,0:T(8,128)S(1)}, u32[]{:S(2)}, u32[]{:S(2)}) %collective-permute-start.9) | collective-permute-done | bytes 24608 | tf_op jit(solution)/shard_map/ppermute | solution.py:80
  27.6 1.2 %shard_map.51 = f32[3,16,512]{2,1,0:T(8,128)} custom-call(f32[48,128]{1,0:T(8,128)S(1)} %get-tuple-element.27.refs_0_, f32[48,128]{1,0:T(8,128)S(1)} %collective-permute-done.7.refs_1_, f32[48,128]{1,0:T(8,128)S(1)} %collective-permute-done.8.refs_2_, f32[48,128]{1,0:T(8,128)S(1)} %collective-permute-done.9.refs_3_, ...), custom_call_target="tpu_custom_call" | custom-call | tf_op jit(solution)/shard_map/pallas_call | solution.py:224
  (1 shorter events, 0.0 us)
Async XLA Ops:
  0.0 0.9 %copy-start.1 = (f32[3,64,64]{2,1,0:T(8,128)S(1)}, f32[3,64,64]{2,1,0:T(8,128)}, u32[]{:S(2)}) copy-start(f32[3,64,64]{2,1,0:T(8,128)} %panel_ref.1) | copy-start | bytes 147460
  0.9 0.8 %copy-start.2 = (f32[64,128]{1,0:T(8,128)S(1)}, f32[64,128]{1,0:T(8,128)}, u32[]{:S(2)}) copy-start(f32[64,128]{1,0:T(8,128)} %tile_ref.1) | copy-start | bytes 98308
  1.7 5.7 %collective-permute-start = (f32[112,128]{1,0:T(8,128)S(1)}, f32[112,128]{1,0:T(8,128)S(1)}, u32[]{:S(2)}, u32[]{:S(2)}) collective-permute-start(f32[112,128]{1,0:T(8,128)S(1)} %get-tuple-element.20), channel_id=1, source_target_pairs={{0,1},{1,0},{2,3},{3,2},{4,5},{5,4},{6,7},{7,6},{8,9},{9,8},{10,11... | collective-permute-start | bytes 172040 | tf_op jit(solution)/shard_map/ppermute | solution.py:80
  4.9 6.2 %collective-permute-start.1 = (f32[112,128]{1,0:T(8,128)S(1)}, f32[112,128]{1,0:T(8,128)S(1)}, u32[]{:S(2)}, u32[]{:S(2)}) collective-permute-start(f32[112,128]{1,0:T(8,128)S(1)} %get-tuple-element.21), channel_id=1, source_target_pairs={{0,2},{1,3},{2,0},{3,1},{4,6},{5,7},{6,4},{7,5},{8,10},{9,11},{10,... | collective-permute-start | bytes 172040 | tf_op jit(solution)/shard_map/ppermute | solution.py:80
  7.4 6.0 %collective-permute-start.2 = (f32[112,128]{1,0:T(8,128)S(1)}, f32[112,128]{1,0:T(8,128)S(1)}, u32[]{:S(2)}, u32[]{:S(2)}) collective-permute-start(f32[112,128]{1,0:T(8,128)S(1)} %get-tuple-element.22), channel_id=1, source_target_pairs={{0,3},{1,2},{2,1},{3,0},{4,7},{5,6},{6,5},{7,4},{8,11},{9,10},{10,... | collective-permute-start | bytes 172040 | tf_op jit(solution)/shard_map/ppermute | solution.py:80
  13.4 3.6 %collective-permute-start.6 = (f32[384,128]{1,0:T(8,128)S(1)}, f32[384,128]{1,0:T(8,128)S(1)}, u32[]{:S(2)}, u32[]{:S(2)}) collective-permute-start(f32[384,128]{1,0:T(8,128)S(1)} %get-tuple-element.24.own_ref), channel_id=1, source_target_pairs={{0,4},{4,0},{8,12},{12,8},{16,20},{20,16},{24,28},{28,24},{1,5},{5... | collective-permute-start | bytes 589832 | tf_op jit(solution)/shard_map/ppermute | solution.py:80
  13.5 5.2 %collective-permute-start.5 = (f32[16,512]{1,0:T(8,128)S(1)}, f32[16,512]{1,0:T(8,128)S(1)}, u32[]{:S(2)}, u32[]{:S(2)}) collective-permute-start(f32[16,512]{1,0:T(8,128)S(1)} %get-tuple-element.23.refs_0_), channel_id=1, source_target_pairs={{0,24},{4,28},{8,16},{12,20},{16,8},{20,12},{24,0},{28,4},{1,25},{... | collective-permute-start | bytes 98312 | tf_op jit(solution)/shard_map/ppermute | solution.py:80
  16.0 3.9 %collective-permute-start.4 = (f32[16,512]{1,0:T(8,128)S(1)}, f32[16,512]{1,0:T(8,128)S(1)}, u32[]{:S(2)}, u32[]{:S(2)}) collective-permute-start(f32[16,512]{1,0:T(8,128)S(1)} %get-tuple-element.23.refs_0_), channel_id=1, source_target_pairs={{0,16},{4,20},{8,24},{12,28},{16,0},{20,4},{24,8},{28,12},{1,17},{... | collective-permute-start | bytes 98312 | tf_op jit(solution)/shard_map/ppermute | solution.py:80
  16.5 3.9 %collective-permute-start.3 = (f32[16,512]{1,0:T(8,128)S(1)}, f32[16,512]{1,0:T(8,128)S(1)}, u32[]{:S(2)}, u32[]{:S(2)}) collective-permute-start(f32[16,512]{1,0:T(8,128)S(1)} %get-tuple-element.23.refs_0_), channel_id=1, source_target_pairs={{0,8},{4,12},{8,0},{12,4},{16,24},{20,28},{24,16},{28,20},{1,9},{5... | collective-permute-start | bytes 98312 | tf_op jit(solution)/shard_map/ppermute | solution.py:80
  17.1 0.7 %copy-start.3 = (s32[3,8]{1,0:T(4,128)S(1)}, s32[3,8]{1,0:T(4,128)}, u32[]{:S(2)}) copy-start(s32[3,8]{1,0:T(4,128)} %block_rows.1) | copy-start | bytes 292
  20.8 5.4 %collective-permute-start.7 = (f32[48,128]{1,0:T(8,128)S(1)}, f32[48,128]{1,0:T(8,128)S(1)}, u32[]{:S(2)}, u32[]{:S(2)}) collective-permute-start(f32[48,128]{1,0:T(8,128)S(1)} %get-tuple-element.28), channel_id=1, source_target_pairs={{0,8},{4,12},{8,0},{12,4},{16,24},{20,28},{24,16},{28,20},{1,9},{5... | collective-permute-start | bytes 73736 | tf_op jit(solution)/shard_map/ppermute | solution.py:80
  21.4 4.9 %collective-permute-start.8 = (f32[48,128]{1,0:T(8,128)S(1)}, f32[48,128]{1,0:T(8,128)S(1)}, u32[]{:S(2)}, u32[]{:S(2)}) collective-permute-start(f32[48,128]{1,0:T(8,128)S(1)} %get-tuple-element.29), channel_id=1, source_target_pairs={{0,16},{4,20},{8,24},{12,28},{16,0},{20,4},{24,8},{28,12},{1,17},{... | collective-permute-start | bytes 73736 | tf_op jit(solution)/shard_map/ppermute | solution.py:80
  22.9 4.7 %collective-permute-start.9 = (f32[48,128]{1,0:T(8,128)S(1)}, f32[48,128]{1,0:T(8,128)S(1)}, u32[]{:S(2)}, u32[]{:S(2)}) collective-permute-start(f32[48,128]{1,0:T(8,128)S(1)} %get-tuple-element.30), channel_id=1, source_target_pairs={{0,24},{4,28},{8,16},{12,20},{16,8},{20,12},{24,0},{28,4},{1,25},{... | collective-permute-start | bytes 73736 | tf_op jit(solution)/shard_map/ppermute | solution.py:80
  24.3 1.6 %copy-start = (f32[2,512,512]{2,1,0:T(8,128)S(1)}, f32[2,512,512]{2,1,0:T(8,128)}, u32[]{:S(2)}) copy-start(f32[2,512,512]{2,1,0:T(8,128)} %couplings.1) | copy-start | bytes 6291460

commit v2 on v1

--- a/solution.py
+++ b/solution.py
@@ -12,6 +12,7 @@
 CORES = 2
 REPLICA_BYTES = 4 << 20
 KERNEL_BYTES = 12 << 20
+ANY = pl.BlockSpec(memory_space=pl.ANY)
 VMEM = pl.BlockSpec(memory_space=pltpu.VMEM)
 SMEM = pl.BlockSpec(memory_space=pltpu.SMEM)
 
@@ -80,18 +81,25 @@
     return lax.ppermute(value, axis, [(i, i ^ distance) for i in range(count)])
 
 
-def pack_kernel(rows, fold, tile_ref, panel_ref, *outs):
+def pack_kernel(rows, fold, tile_hbm, panel_hbm, *refs):
+    *outs, tile, panel, tile_done, panel_done = refs
     column = lax.axis_index("col")
-    high = panel_ref.shape[1] // fold
-    for section in range(panel_ref.shape[0]):
+    tile_copy = pltpu.make_async_copy(tile_hbm, tile, tile_done)
+    panel_copy = pltpu.make_async_copy(panel_hbm, panel, panel_done)
+    panel_copy.start()
+    tile_copy.start()
+    high = panel.shape[1] // fold
+    tile_copy.wait()
+    for away, out in enumerate(outs):
+        start = pl.multiple_of((column ^ away) * rows, rows)
+        out[panel.shape[0] * high :, :] = tile[pl.ds(start, rows), :]
+    panel_copy.wait()
+    for section in range(panel.shape[0]):
         dense = jnp.concatenate(
-            [panel_ref[section, i * high : (i + 1) * high, :] for i in range(fold)], axis=1
+            [panel[section, i * high : (i + 1) * high, :] for i in range(fold)], axis=1
         )
         for out in outs:
             out[section * high : (section + 1) * high, :] = dense
-    for away, out in enumerate(outs):
-        start = pl.multiple_of((column ^ away) * rows, rows)
-        out[panel_ref.shape[0] * high :, :] = tile_ref[pl.ds(start, rows), :]
 
 
 def join_kernel(*refs):
@@ -202,8 +210,14 @@
     packed = call(
         functools.partial(pack_kernel, rows, fold),
         [jax.ShapeDtypeStruct((depth + rows, LANES), f32)] * cols,
-        [VMEM, VMEM],
-    )(inverse_tiles, factor_panels)
+        [ANY, ANY],
+        [
+            pltpu.VMEM(inverse_tiles.shape, f32),
+            pltpu.VMEM(factor_panels.shape, f32),
+            pltpu.SemaphoreType.DMA,
+            pltpu.SemaphoreType.DMA,
+        ],
+    )(*[pltpu.with_memory_space_constraint(x, pltpu.HBM) for x in (inverse_tiles, factor_panels)])
     arrived = [packed[0]] + [swap(packed[away], "col", away) for away in range(1, cols)]
     inverse, line = call(
         join_kernel,

time: 29 us -> 28.2 us (0.972)
  local copies, waits for them, and re-layouts: 3.92 us -> 2.27 us
  Pallas kernels: 2.76 us -> 3.67 us
    unnamed x8 -> x4, local copies, waits for them, and re-layouts: 3.92 us -> 2.27 us
    pallas_call x1, Pallas kernels: 0.08 us -> 0.99 us  [gathered(): call(functools.partial(pack_kernel, rows, fold), [jax.ShapeDtypeStruct((d...]
where the time goes in v2:
time: 28.2 us; the launch traced here: 28 us
  starting transfers between devices  12.9 us (46%)
  waiting for transfers between devices  9.14 us (32%)
  Pallas kernels  3.67 us (13%)
  local copies, waits for them, and re-layouts  2.27 us (8%)
    ppermute x10, starting transfers between devices, swap(): return lax.ppermute(value, axis, [(i, i ^ distance) for i in range(count)])  12.9 us
    ppermute x10, waiting for transfers between devices, swap(): return lax.ppermute(value, axis, [(i, i ^ distance) for i in range(count)])  9.14 us
    unnamed x4, local copies, waits for them, and re-layouts  2.27 us
    pallas_call x1, Pallas kernels, gathered(): call(finish_kernel, jax.ShapeDtypeStruct((sections, rows, piece_rows * co...  1.17 us
    pallas_call x1, Pallas kernels, gathered(): call(functools.partial(pack_kernel, rows, fold), [jax.ShapeDtypeStruct((d...  0.99 us
    pallas_call x1, Pallas kernels, gathered(): call(functools.partial(place_kernel, fold, LANES // block_size, listed //...  0.9 us
  transfers between devices with their start and end apart: 10, of which 5 were waited for; matrix products, arithmetic and copies ran while one was open for 0% of the time, Pallas kernels for 4%

profile of v2, /device:TPU:0, one launch (start us, length us, event | category | flops | bytes accessed | tf_op | source)
XLA Modules:
  0.0 28.0 jit_solution(3672299154635723823)
XLA Ops:
  0.0 1.0 %shard_map.46 = (f32[112,128]{1,0:T(8,128)S(1)}, f32[112,128]{1,0:T(8,128)S(1)}, f32[112,128]{1,0:T(8,128)S(1)}, f32[112,128]{1,0:T(8,128)S(1)}) custom-call(f32[64,128]{1,0:T(8,128)} %tile_hbm.1, f32[3,64,64]{2,1,0:T(8,128)} %panel_hbm.1), custom_call_target="tpu_custom_call" | custom-call | tf_op jit(solution)/shard_map/pallas_call | solution.py:210
  1.0 3.1 %collective-permute-start = (f32[112,128]{1,0:T(8,128)S(1)}, f32[112,128]{1,0:T(8,128)S(1)}, u32[]{:S(2)}, u32[]{:S(2)}) collective-permute-start(f32[112,128]{1,0:T(8,128)S(1)} %get-tuple-element.20), channel_id=1, source_target_pairs={{0,1},{1,0},{2,3},{3,2},{4,5},{5,4},{6,7},{7,6},{8,9},{9,8},{10,11... | collective-permute-start | bytes 172040 | tf_op jit(solution)/shard_map/ppermute | solution.py:81
  4.1 2.6 %collective-permute-start.1 = (f32[112,128]{1,0:T(8,128)S(1)}, f32[112,128]{1,0:T(8,128)S(1)}, u32[]{:S(2)}, u32[]{:S(2)}) collective-permute-start(f32[112,128]{1,0:T(8,128)S(1)} %get-tuple-element.21), channel_id=1, source_target_pairs={{0,2},{1,3},{2,0},{3,1},{4,6},{5,7},{6,4},{7,5},{8,10},{9,11},{10,... | collective-permute-start | bytes 172040 | tf_op jit(solution)/shard_map/ppermute | solution.py:81
  6.7 0.0 collective-permute-start.2
  6.7 0.0 collective-permute-done.refs_1_
  6.7 3.6 %collective-permute-done.1.refs_2_ = f32[112,128]{1,0:T(8,128)S(1)} collective-permute-done((f32[112,128]{1,0:T(8,128)S(1)}, f32[112,128]{1,0:T(8,128)S(1)}, u32[]{:S(2)}, u32[]{:S(2)}) %collective-permute-start.1) | collective-permute-done | bytes 57376 | tf_op jit(solution)/shard_map/ppermute | solution.py:81
  10.3 2.4 %collective-permute-done.2.refs_3_ = f32[112,128]{1,0:T(8,128)S(1)} collective-permute-done((f32[112,128]{1,0:T(8,128)S(1)}, f32[112,128]{1,0:T(8,128)S(1)}, u32[]{:S(2)}, u32[]{:S(2)}) %collective-permute-start.2) | collective-permute-done | bytes 57376 | tf_op jit(solution)/shard_map/ppermute | solution.py:81
  12.7 0.1 collective-permute-start.6
  12.8 2.5 %collective-permute-start.5 = (f32[16,512]{1,0:T(8,128)S(1)}, f32[16,512]{1,0:T(8,128)S(1)}, u32[]{:S(2)}, u32[]{:S(2)}) collective-permute-start(f32[16,512]{1,0:T(8,128)S(1)} %get-tuple-element.23.refs_0_), channel_id=1, source_target_pairs={{0,24},{4,28},{8,16},{12,20},{16,8},{20,12},{24,0},{28,4},{1,25},{... | collective-permute-start | bytes 98312 | tf_op jit(solution)/shard_map/ppermute | solution.py:81
  15.3 0.5 %collective-permute-start.4 = (f32[16,512]{1,0:T(8,128)S(1)}, f32[16,512]{1,0:T(8,128)S(1)}, u32[]{:S(2)}, u32[]{:S(2)}) collective-permute-start(f32[16,512]{1,0:T(8,128)S(1)} %get-tuple-element.23.refs_0_), channel_id=1, source_target_pairs={{0,16},{4,20},{8,24},{12,28},{16,0},{20,4},{24,8},{28,12},{1,17},{... | collective-permute-start | bytes 98312 | tf_op jit(solution)/shard_map/ppermute | solution.py:81
  15.8 0.5 %collective-permute-start.3 = (f32[16,512]{1,0:T(8,128)S(1)}, f32[16,512]{1,0:T(8,128)S(1)}, u32[]{:S(2)}, u32[]{:S(2)}) collective-permute-start(f32[16,512]{1,0:T(8,128)S(1)} %get-tuple-element.23.refs_0_), channel_id=1, source_target_pairs={{0,8},{4,12},{8,0},{12,4},{16,24},{20,28},{24,16},{28,20},{1,9},{5... | collective-permute-start | bytes 98312 | tf_op jit(solution)/shard_map/ppermute | solution.py:81
  16.3 0.0 collective-permute-done.6.other_ref
  16.3 0.0 copy-start.1
  16.3 0.7 %copy-done.1 = s32[3,8]{1,0:T(4,128)S(1)} copy-done((s32[3,8]{1,0:T(4,128)S(1)}, s32[3,8]{1,0:T(4,128)}, u32[]{:S(2)}) %copy-start.1) | copy-done | bytes 120
  17.0 0.9 %shard_map.48 = (bf16[512,384]{1,0:T(8,128)(2,1)S(1)}, bf16[512,384]{1,0:T(8,128)(2,1)S(1)}) custom-call(s32[3,8]{1,0:T(4,128)S(1)} %copy-done.1, f32[384,128]{1,0:T(8,128)S(1)} %get-tuple-element.24.own_ref, f32[384,128]{1,0:T(8,128)S(1)} %collective-permute-done.6.other_ref), custom_call_target="tpu_custom_call" | custom-call | tf_op jit(solution)/shard_map/pallas_call | solution.py:228
  17.9 0.0 collective-permute-done.5.refs_3_
  17.9 1.3 %collective-permute-done.4.refs_2_ = f32[16,512]{1,0:T(8,128)S(1)} collective-permute-done((f32[16,512]{1,0:T(8,128)S(1)}, f32[16,512]{1,0:T(8,128)S(1)}, u32[]{:S(2)}, u32[]{:S(2)}) %collective-permute-start.4) | collective-permute-done | bytes 32800 | tf_op jit(solution)/shard_map/ppermute | solution.py:81
  19.2 0.5 %collective-permute-done.3.refs_1_ = f32[16,512]{1,0:T(8,128)S(1)} collective-permute-done((f32[16,512]{1,0:T(8,128)S(1)}, f32[16,512]{1,0:T(8,128)S(1)}, u32[]{:S(2)}, u32[]{:S(2)}) %collective-permute-start.3) | collective-permute-done | bytes 32800 | tf_op jit(solution)/shard_map/ppermute | solution.py:81
  19.7 0.3 %shard_map.49 = (f32[48,128]{1,0:T(8,128)S(1)}, f32[48,128]{1,0:T(8,128)S(1)}, f32[48,128]{1,0:T(8,128)S(1)}, f32[48,128]{1,0:T(8,128)S(1)}) custom-call(f32[16,512]{1,0:T(8,128)S(1)} %get-tuple-element.23.refs_0_, f32[16,512]{1,0:T(8,128)S(1)} %collective-permute-done.3.refs_1_, f32[16,512]{1,0:T(8,128)S(1)} %collective-permute-done.4.refs_2_, ...), custom_call_target="tpu_custom_call" | custom-call | tf_op jit(solution)/shard_map/pallas_call | solution.py:233
  20.0 0.6 %collective-permute-start.7 = (f32[48,128]{1,0:T(8,128)S(1)}, f32[48,128]{1,0:T(8,128)S(1)}, u32[]{:S(2)}, u32[]{:S(2)}) collective-permute-start(f32[48,128]{1,0:T(8,128)S(1)} %get-tuple-element.28), channel_id=1, source_target_pairs={{0,8},{4,12},{8,0},{12,4},{16,24},{20,28},{24,16},{28,20},{1,9},{5... | collective-permute-start | bytes 73736 | tf_op jit(solution)/shard_map/ppermute | solution.py:81
  20.6 1.5 %collective-permute-start.8 = (f32[48,128]{1,0:T(8,128)S(1)}, f32[48,128]{1,0:T(8,128)S(1)}, u32[]{:S(2)}, u32[]{:S(2)}) collective-permute-start(f32[48,128]{1,0:T(8,128)S(1)} %get-tuple-element.29), channel_id=1, source_target_pairs={{0,16},{4,20},{8,24},{12,28},{16,0},{20,4},{24,8},{28,12},{1,17},{... | collective-permute-start | bytes 73736 | tf_op jit(solution)/shard_map/ppermute | solution.py:81
  22.1 1.4 %collective-permute-start.9 = (f32[48,128]{1,0:T(8,128)S(1)}, f32[48,128]{1,0:T(8,128)S(1)}, u32[]{:S(2)}, u32[]{:S(2)}) collective-permute-start(f32[48,128]{1,0:T(8,128)S(1)} %get-tuple-element.30), channel_id=1, source_target_pairs={{0,24},{4,28},{8,16},{12,20},{16,8},{20,12},{24,0},{28,4},{1,25},{... | collective-permute-start | bytes 73736 | tf_op jit(solution)/shard_map/ppermute | solution.py:81
  23.6 0.0 copy-start
  23.6 1.6 %copy-done = f32[2,512,512]{2,1,0:T(8,128)S(1)} copy-done((f32[2,512,512]{2,1,0:T(8,128)S(1)}, f32[2,512,512]{2,1,0:T(8,128)}, u32[]{:S(2)}) %copy-start) | copy-done | bytes 2097176
  25.2 0.3 %shard_map.50 = (bf16[2,512,512]{2,1,0:T(8,128)(2,1)S(1)}, bf16[2,512,512]{2,1,0:T(8,128)(2,1)S(1)}) custom-call(f32[2,512,512]{2,1,0:T(8,128)S(1)} %copy-done), custom_call_target="tpu_custom_call" | custom-call | tf_op jit(solution)/shard_map/pallas_call | solution.py:237
  25.5 0.0 collective-permute-done.7.refs_1_
  25.5 0.0 collective-permute-done.8.refs_2_
  25.5 1.4 %collective-permute-done.9.refs_3_ = f32[48,128]{1,0:T(8,128)S(1)} collective-permute-done((f32[48,128]{1,0:T(8,128)S(1)}, f32[48,128]{1,0:T(8,128)S(1)}, u32[]{:S(2)}, u32[]{:S(2)}) %collective-permute-start.9) | collective-permute-done | bytes 24608 | tf_op jit(solution)/shard_map/ppermute | solution.py:81
  26.9 1.2 %shard_map.51 = f32[3,16,512]{2,1,0:T(8,128)} custom-call(f32[48,128]{1,0:T(8,128)S(1)} %get-tuple-element.27.refs_0_, f32[48,128]{1,0:T(8,128)S(1)} %collective-permute-done.7.refs_1_, f32[48,128]{1,0:T(8,128)S(1)} %collective-permute-done.8.refs_2_, f32[48,128]{1,0:T(8,128)S(1)} %collective-permute-done.9.refs_3_, ...), custom_call_target="tpu_custom_call" | custom-call | tf_op jit(solution)/shard_map/pallas_call | solution.py:238
  (1 shorter events, 0.0 us)
Async XLA Ops:
  1.0 5.7 %collective-permute-start = (f32[112,128]{1,0:T(8,128)S(1)}, f32[112,128]{1,0:T(8,128)S(1)}, u32[]{:S(2)}, u32[]{:S(2)}) collective-permute-start(f32[112,128]{1,0:T(8,128)S(1)} %get-tuple-element.20), channel_id=1, source_target_pairs={{0,1},{1,0},{2,3},{3,2},{4,5},{5,4},{6,7},{7,6},{8,9},{9,8},{10,11... | collective-permute-start | bytes 172040 | tf_op jit(solution)/shard_map/ppermute | solution.py:81
  4.1 6.2 %collective-permute-start.1 = (f32[112,128]{1,0:T(8,128)S(1)}, f32[112,128]{1,0:T(8,128)S(1)}, u32[]{:S(2)}, u32[]{:S(2)}) collective-permute-start(f32[112,128]{1,0:T(8,128)S(1)} %get-tuple-element.21), channel_id=1, source_target_pairs={{0,2},{1,3},{2,0},{3,1},{4,6},{5,7},{6,4},{7,5},{8,10},{9,11},{10,... | collective-permute-start | bytes 172040 | tf_op jit(solution)/shard_map/ppermute | solution.py:81
  6.7 6.0 %collective-permute-start.2 = (f32[112,128]{1,0:T(8,128)S(1)}, f32[112,128]{1,0:T(8,128)S(1)}, u32[]{:S(2)}, u32[]{:S(2)}) collective-permute-start(f32[112,128]{1,0:T(8,128)S(1)} %get-tuple-element.22), channel_id=1, source_target_pairs={{0,3},{1,2},{2,1},{3,0},{4,7},{5,6},{6,5},{7,4},{8,11},{9,10},{10,... | collective-permute-start | bytes 172040 | tf_op jit(solution)/shard_map/ppermute | solution.py:81
  12.7 3.6 %collective-permute-start.6 = (f32[384,128]{1,0:T(8,128)S(1)}, f32[384,128]{1,0:T(8,128)S(1)}, u32[]{:S(2)}, u32[]{:S(2)}) collective-permute-start(f32[384,128]{1,0:T(8,128)S(1)} %get-tuple-element.24.own_ref), channel_id=1, source_target_pairs={{0,4},{4,0},{8,12},{12,8},{16,20},{20,16},{24,28},{28,24},{1,5},{5... | collective-permute-start | bytes 589832 | tf_op jit(solution)/shard_map/ppermute | solution.py:81
  12.8 5.2 %collective-permute-start.5 = (f32[16,512]{1,0:T(8,128)S(1)}, f32[16,512]{1,0:T(8,128)S(1)}, u32[]{:S(2)}, u32[]{:S(2)}) collective-permute-start(f32[16,512]{1,0:T(8,128)S(1)} %get-tuple-element.23.refs_0_), channel_id=1, source_target_pairs={{0,24},{4,28},{8,16},{12,20},{16,8},{20,12},{24,0},{28,4},{1,25},{... | collective-permute-start | bytes 98312 | tf_op jit(solution)/shard_map/ppermute | solution.py:81
  15.3 3.9 %collective-permute-start.4 = (f32[16,512]{1,0:T(8,128)S(1)}, f32[16,512]{1,0:T(8,128)S(1)}, u32[]{:S(2)}, u32[]{:S(2)}) collective-permute-start(f32[16,512]{1,0:T(8,128)S(1)} %get-tuple-element.23.refs_0_), channel_id=1, source_target_pairs={{0,16},{4,20},{8,24},{12,28},{16,0},{20,4},{24,8},{28,12},{1,17},{... | collective-permute-start | bytes 98312 | tf_op jit(solution)/shard_map/ppermute | solution.py:81
  15.8 3.9 %collective-permute-start.3 = (f32[16,512]{1,0:T(8,128)S(1)}, f32[16,512]{1,0:T(8,128)S(1)}, u32[]{:S(2)}, u32[]{:S(2)}) collective-permute-start(f32[16,512]{1,0:T(8,128)S(1)} %get-tuple-element.23.refs_0_), channel_id=1, source_target_pairs={{0,8},{4,12},{8,0},{12,4},{16,24},{20,28},{24,16},{28,20},{1,9},{5... | collective-permute-start | bytes 98312 | tf_op jit(solution)/shard_map/ppermute | solution.py:81
  16.3 0.7 %copy-start.1 = (s32[3,8]{1,0:T(4,128)S(1)}, s32[3,8]{1,0:T(4,128)}, u32[]{:S(2)}) copy-start(s32[3,8]{1,0:T(4,128)} %block_rows.1) | copy-start | bytes 292
  20.0 5.4 %collective-permute-start.7 = (f32[48,128]{1,0:T(8,128)S(1)}, f32[48,128]{1,0:T(8,128)S(1)}, u32[]{:S(2)}, u32[]{:S(2)}) collective-permute-start(f32[48,128]{1,0:T(8,128)S(1)} %get-tuple-element.28), channel_id=1, source_target_pairs={{0,8},{4,12},{8,0},{12,4},{16,24},{20,28},{24,16},{28,20},{1,9},{5... | collective-permute-start | bytes 73736 | tf_op jit(solution)/shard_map/ppermute | solution.py:81
  20.6 4.9 %collective-permute-start.8 = (f32[48,128]{1,0:T(8,128)S(1)}, f32[48,128]{1,0:T(8,128)S(1)}, u32[]{:S(2)}, u32[]{:S(2)}) collective-permute-start(f32[48,128]{1,0:T(8,128)S(1)} %get-tuple-element.29), channel_id=1, source_target_pairs={{0,16},{4,20},{8,24},{12,28},{16,0},{20,4},{24,8},{28,12},{1,17},{... | collective-permute-start | bytes 73736 | tf_op jit(solution)/shard_map/ppermute | solution.py:81
  22.1 4.7 %collective-permute-start.9 = (f32[48,128]{1,0:T(8,128)S(1)}, f32[48,128]{1,0:T(8,128)S(1)}, u32[]{:S(2)}, u32[]{:S(2)}) collective-permute-start(f32[48,128]{1,0:T(8,128)S(1)} %get-tuple-element.30), channel_id=1, source_target_pairs={{0,24},{4,28},{8,16},{12,20},{16,8},{20,12},{24,0},{28,4},{1,25},{... | collective-permute-start | bytes 73736 | tf_op jit(solution)/shard_map/ppermute | solution.py:81
  23.6 1.6 %copy-start = (f32[2,512,512]{2,1,0:T(8,128)S(1)}, f32[2,512,512]{2,1,0:T(8,128)}, u32[]{:S(2)}) copy-start(f32[2,512,512]{2,1,0:T(8,128)} %couplings.1) | copy-start | bytes 6291460

commit v3 on v2

--- a/solution.py
+++ b/solution.py
@@ -76,9 +76,9 @@
     return high, (value - high.astype(jnp.float32)).astype(jnp.bfloat16)
 
 
-def swap(value, axis, distance):
-    count = lax.axis_size(axis)
-    return lax.ppermute(value, axis, [(i, i ^ distance) for i in range(count)])
+def swap(value, axis, distances):
+    pairs = [(i, i ^ distances[i % len(distances)]) for i in range(lax.axis_size(axis))]
+    return lax.ppermute(value, axis, pairs)
 
 
 def pack_kernel(rows, fold, tile_hbm, panel_hbm, *refs):
@@ -108,6 +108,13 @@
     for away, part in enumerate(parts):
         inverse[:, away * LANES : (away + 1) * LANES] = part[depth:, :]
         line[away * depth : (away + 1) * depth, :] = part[:depth, :]
+
+
+def both_kernel(own, other, out):
+    rows = own.shape[0]
+    core = lax.rem(lax.axis_index("row"), CORES)
+    out[pl.ds(pl.multiple_of(core * rows, rows), rows), :] = own[...]
+    out[pl.ds(pl.multiple_of((CORES - 1 - core) * rows, rows), rows), :] = other[...]
 
 
 def couplings_kernel(couplings, high_ref, low_ref):
@@ -165,20 +172,38 @@
     rows = inverses[0].shape[0]
     stacked = jnp.concatenate(split(jnp.concatenate([ref[...] for ref in inverses], axis=0)), axis=0)
     total = product(stacked, high_ref[...], low_ref[...])
-    for chip, out in enumerate(outs):
-        for section in range(total.shape[1] // LANES):
-            out[section * rows : (section + 1) * rows, :] = total[
-                chip * rows : (chip + 1) * rows, section * LANES : (section + 1) * LANES
-            ]
-
-
-def finish_kernel(*refs):
-    *parts, high_ref, low_ref, out = refs
+    sections = total.shape[1] // LANES
+    start = 0
+    for out in outs:
+        for at in range(0, out.shape[0], rows):
+            section = at // rows % sections
+            out[at : at + rows, :] = total[start : start + rows, section * LANES : (section + 1) * LANES]
+            if section == sections - 1:
+                start += rows
+
+
+def other_kernel(pair, out):
+    size = out.shape[0]
+    core = lax.rem(lax.axis_index("row"), CORES)
+    out[...] = pair[pl.ds(pl.multiple_of((CORES - 1 - core) * size, size), size), :]
+
+
+def finish_kernel(own, near, far, handed, high_ref, low_ref, out):
     sections, rows, _ = out.shape
     chip = lax.div(lax.axis_index("row"), CORES)
+    core = lax.rem(lax.axis_index("row"), CORES)
+    size = sections * rows
     previous = None
     for section in range(sections):
-        tiles = [part[section * rows : (section + 1) * rows, :] for part in parts]
+        at = section * rows
+        kept = far[pl.ds(pl.multiple_of(core * size + at, rows), rows), :]
+        given = handed[at : at + rows, :]
+        tiles = [
+            own[at : at + rows, :],
+            jnp.where(core == 0, kept, given),
+            near[at : at + rows, :],
+            jnp.where(core == 0, given, kept),
+        ]
         step = 1
         while step < len(tiles):
             tiles = [
@@ -205,7 +230,8 @@
     depth = sections * piece_rows // fold
 
     bf16 = jnp.bfloat16
-    chips = range(0, count, CORES)
+    beside, along, across = ([CORES * i] for i in (1, 2, 3))
+    pair, far = [1], beside + across
 
     packed = call(
         functools.partial(pack_kernel, rows, fold),
@@ -218,26 +244,34 @@
             pltpu.SemaphoreType.DMA,
         ],
     )(*[pltpu.with_memory_space_constraint(x, pltpu.HBM) for x in (inverse_tiles, factor_panels)])
-    arrived = [packed[0]] + [swap(packed[away], "col", away) for away in range(1, cols)]
+    arrived = [packed[0]] + [swap(packed[away], "col", [away]) for away in range(1, cols)]
     inverse, line = call(
         join_kernel,
         [jax.ShapeDtypeStruct((rows, order), f32), jax.ShapeDtypeStruct((cols * depth, LANES), f32)],
         [VMEM] * cols,
     )(*arrived)
-    inverses = [inverse] + [swap(inverse, "row", chip) for chip in chips[1:]]
+    other, other_line = swap(inverse, "row", pair), swap(line, "row", pair)
+    both = call(both_kernel, jax.ShapeDtypeStruct((CORES * rows, order), f32), [VMEM, VMEM])(inverse, other)
+    inverses = [inverse, swap(inverse, "row", along), swap(both, "row", far)]
     placed = call(
         functools.partial(place_kernel, fold, LANES // block_size, listed // cols, block_size),
         [jax.ShapeDtypeStruct((order, sections * LANES), bf16)] * 2,
         [SMEM, VMEM, VMEM],
-    )(block_rows, line, swap(line, "row", 1))
-    products = call(
-        multiply_kernel, [jax.ShapeDtypeStruct((sections * rows, LANES), f32)] * len(chips), [VMEM] * (len(chips) + 2)
+    )(block_rows, line, other_line)
+    own, to_near, to_far = call(
+        multiply_kernel,
+        [jax.ShapeDtypeStruct((n * sections * rows, LANES), f32) for n in (1, 1, CORES)],
+        [VMEM] * (len(inverses) + 2),
     )(*inverses, *placed)
-    returned = [products[0]] + [swap(products[i], "row", chip) for i, chip in enumerate(chips) if chip]
+    from_far = swap(to_far, "row", far)
+    from_near = swap(to_near, "row", along)
+    handed = swap(
+        call(other_kernel, jax.ShapeDtypeStruct((sections * rows, LANES), f32), [VMEM])(from_far), "row", pair
+    )
     halves = call(couplings_kernel, [jax.ShapeDtypeStruct(couplings.shape, bf16)] * 2, [VMEM])(couplings)
     return call(
-        finish_kernel, jax.ShapeDtypeStruct((sections, rows, piece_rows * count), f32), [VMEM] * (len(chips) + 2)
-    )(*returned, *halves)
+        finish_kernel, jax.ShapeDtypeStruct((sections, rows, piece_rows * count), f32), [VMEM] * 6
+    )(own, from_near, from_far, handed, *halves)
 
 
 def on_device(inverse_tiles, factor_panels, block_rows, couplings):
@@ -246,7 +280,8 @@
     powers = all(n & (n - 1) == 0 for n in (count, cols))
     fits = sections * piece_rows * width * count * cols * 4 <= REPLICA_BYTES
     lanes = inverse_tiles.shape[1] == LANES == CORES * piece_rows and LANES % width == 0
-    if powers and fits and lanes and count % CORES == 0 == cols % (LANES // width):
+    square = count == 4 * CORES
+    if powers and fits and lanes and square and cols % (LANES // width) == 0:
         return gathered(inverse_tiles, factor_panels, block_rows, couplings)
     return streamed(inverse_tiles, factor_panels, block_rows, couplings)
 

time: 28.2 us -> 27.8 us (0.986)
  starting transfers between devices: 12.9 us -> 11.5 us
  waiting for transfers between devices: 9.14 us -> 10.1 us
    ppermute x10, starting transfers between devices: 12.9 us -> 11.5 us  [swap(): return lax.ppermute(value, axis, pairs)]
    ppermute x10, waiting for transfers between devices: 9.14 us -> 10.1 us  [swap(): return lax.ppermute(value, axis, pairs)]
where the time goes in v3:
time: 27.8 us; the launch traced here: 27.6 us
  starting transfers between devices  11.5 us (41%)
  waiting for transfers between devices  10.1 us (36%)
  Pallas kernels  3.68 us (13%)
  local copies, waits for them, and re-layouts  2.27 us (8%)
    ppermute x10, starting transfers between devices, swap(): return lax.ppermute(value, axis, pairs)  11.5 us
    ppermute x10, waiting for transfers between devices, swap(): return lax.ppermute(value, axis, pairs)  10.1 us
    unnamed x4, local copies, waits for them, and re-layouts  2.27 us
    pallas_call x1, Pallas kernels, gathered(): call(finish_kernel, jax.ShapeDtypeStruct((sections, rows, piece_rows * co...  1.17 us
    pallas_call x1, Pallas kernels, gathered(): call(functools.partial(pack_kernel, rows, fold), [jax.ShapeDtypeStruct((d...  0.99 us
    pallas_call x1, Pallas kernels, gathered(): call(functools.partial(place_kernel, fold, LANES // block_size, listed //...  0.9 us
  transfers between devices with their start and end apart: 10, of which 5 were waited for; matrix products, arithmetic and copies ran while one was open for 0% of the time, Pallas kernels for 4%

profile of v3, /device:TPU:0, one launch (start us, length us, event | category | flops | bytes accessed | tf_op | source)
XLA Modules:
  0.0 27.6 jit_solution(602769104664959037)
XLA Ops:
  0.0 1.0 %shard_map.46 = (f32[112,128]{1,0:T(8,128)S(1)}, f32[112,128]{1,0:T(8,128)S(1)}, f32[112,128]{1,0:T(8,128)S(1)}, f32[112,128]{1,0:T(8,128)S(1)}) custom-call(f32[64,128]{1,0:T(8,128)} %tile_hbm.1, f32[3,64,64]{2,1,0:T(8,128)} %panel_hbm.1), custom_call_target="tpu_custom_call" | custom-call | tf_op jit(solution)/shard_map/pallas_call | solution.py:236
  1.0 3.1 %collective-permute-start = (f32[112,128]{1,0:T(8,128)S(1)}, f32[112,128]{1,0:T(8,128)S(1)}, u32[]{:S(2)}, u32[]{:S(2)}) collective-permute-start(f32[112,128]{1,0:T(8,128)S(1)} %get-tuple-element.19), channel_id=1, source_target_pairs={{0,1},{1,0},{2,3},{3,2},{4,5},{5,4},{6,7},{7,6},{8,9},{9,8},{10,11... | collective-permute-start | bytes 172040 | tf_op jit(solution)/shard_map/ppermute | solution.py:81
  4.1 2.6 %collective-permute-start.1 = (f32[112,128]{1,0:T(8,128)S(1)}, f32[112,128]{1,0:T(8,128)S(1)}, u32[]{:S(2)}, u32[]{:S(2)}) collective-permute-start(f32[112,128]{1,0:T(8,128)S(1)} %get-tuple-element.20), channel_id=1, source_target_pairs={{0,2},{1,3},{2,0},{3,1},{4,6},{5,7},{6,4},{7,5},{8,10},{9,11},{10,... | collective-permute-start | bytes 172040 | tf_op jit(solution)/shard_map/ppermute | solution.py:81
  6.7 0.0 collective-permute-start.2
  6.7 0.0 collective-permute-done.refs_1_
  6.7 3.6 %collective-permute-done.1.refs_2_ = f32[112,128]{1,0:T(8,128)S(1)} collective-permute-done((f32[112,128]{1,0:T(8,128)S(1)}, f32[112,128]{1,0:T(8,128)S(1)}, u32[]{:S(2)}, u32[]{:S(2)}) %collective-permute-start.1) | collective-permute-done | bytes 57376 | tf_op jit(solution)/shard_map/ppermute | solution.py:81
  10.3 2.4 %collective-permute-done.2.refs_3_ = f32[112,128]{1,0:T(8,128)S(1)} collective-permute-done((f32[112,128]{1,0:T(8,128)S(1)}, f32[112,128]{1,0:T(8,128)S(1)}, u32[]{:S(2)}, u32[]{:S(2)}) %collective-permute-start.2) | collective-permute-done | bytes 57376 | tf_op jit(solution)/shard_map/ppermute | solution.py:81
  12.7 0.1 collective-permute-start.6
  12.8 0.5 %collective-permute-start.4 = (f32[16,512]{1,0:T(8,128)S(1)}, f32[16,512]{1,0:T(8,128)S(1)}, u32[]{:S(2)}, u32[]{:S(2)}) collective-permute-start(f32[16,512]{1,0:T(8,128)S(1)} %get-tuple-element.22.own.refs_0_), channel_id=1, source_target_pairs={{0,4},{4,0},{8,12},{12,8},{16,20},{20,16},{24,28},{28,24},{1,5},{5... | collective-permute-start | bytes 98312 | tf_op jit(solution)/shard_map/ppermute | solution.py:81
  13.3 1.0 %collective-permute-done.4.other = f32[16,512]{1,0:T(8,128)S(1)} collective-permute-done((f32[16,512]{1,0:T(8,128)S(1)}, f32[16,512]{1,0:T(8,128)S(1)}, u32[]{:S(2)}, u32[]{:S(2)}) %collective-permute-start.4) | collective-permute-done | bytes 32800 | tf_op jit(solution)/shard_map/ppermute | solution.py:81
  14.3 1.6 %collective-permute-start.5 = (f32[32,512]{1,0:T(8,128)S(1)}, f32[32,512]{1,0:T(8,128)S(1)}, u32[]{:S(2)}, u32[]{:S(2)}) collective-permute-start(f32[32,512]{1,0:T(8,128)S(1)} %shard_map.48), channel_id=1, source_target_pairs={{0,8},{4,28},{8,0},{12,20},{16,24},{20,12},{24,16},{28,4},{1,9},{5... | collective-permute-start | bytes 196616 | tf_op jit(solution)/shard_map/ppermute | solution.py:81
  15.8 1.5 %collective-permute-start.3 = (f32[16,512]{1,0:T(8,128)S(1)}, f32[16,512]{1,0:T(8,128)S(1)}, u32[]{:S(2)}, u32[]{:S(2)}) collective-permute-start(f32[16,512]{1,0:T(8,128)S(1)} %get-tuple-element.22.own.refs_0_), channel_id=1, source_target_pairs={{0,16},{4,20},{8,24},{12,28},{16,0},{20,4},{24,8},{28,12},{1,17},{... | collective-permute-start | bytes 98312 | tf_op jit(solution)/shard_map/ppermute | solution.py:81
  17.3 0.0 collective-permute-done.6.other_ref
  17.3 0.0 copy-start.1
  17.3 0.7 %copy-done.1 = s32[3,8]{1,0:T(4,128)S(1)} copy-done((s32[3,8]{1,0:T(4,128)S(1)}, s32[3,8]{1,0:T(4,128)}, u32[]{:S(2)}) %copy-start.1) | copy-done | bytes 120
  18.0 0.9 %shard_map.49 = (bf16[512,384]{1,0:T(8,128)(2,1)S(1)}, bf16[512,384]{1,0:T(8,128)(2,1)S(1)}) custom-call(s32[3,8]{1,0:T(4,128)S(1)} %copy-done.1, f32[384,128]{1,0:T(8,128)S(1)} %get-tuple-element.23.own_ref, f32[384,128]{1,0:T(8,128)S(1)} %collective-permute-done.6.other_ref), custom_call_target="tpu_custom_call" | custom-call | tf_op jit(solution)/shard_map/pallas_call | solution.py:256
  18.9 1.1 %collective-permute-done.3.refs_1_ = f32[16,512]{1,0:T(8,128)S(1)} collective-permute-done((f32[16,512]{1,0:T(8,128)S(1)}, f32[16,512]{1,0:T(8,128)S(1)}, u32[]{:S(2)}, u32[]{:S(2)}) %collective-permute-start.3) | collective-permute-done | bytes 32800 | tf_op jit(solution)/shard_map/ppermute | solution.py:81
  20.0 0.0 collective-permute-done.5.refs_2_
  20.0 0.3 %shard_map.50 = (f32[48,128]{1,0:T(8,128)S(1)}, f32[48,128]{1,0:T(8,128)S(1)}, f32[96,128]{1,0:T(8,128)S(1)}) custom-call(f32[16,512]{1,0:T(8,128)S(1)} %get-tuple-element.22.own.refs_0_, f32[16,512]{1,0:T(8,128)S(1)} %collective-permute-done.3.refs_1_, f32[32,512]{1,0:T(8,128)S(1)} %collective-permute-done.5.refs_2_, ...), custom_call_target="tpu_custom_call" | custom-call | tf_op jit(solution)/shard_map/pallas_call | solution.py:261
  20.3 1.0 %collective-permute-start.8 = (f32[96,128]{1,0:T(8,128)S(1)}, f32[96,128]{1,0:T(8,128)S(1)}, u32[]{:S(2)}, u32[]{:S(2)}) collective-permute-start(f32[96,128]{1,0:T(8,128)S(1)} %get-tuple-element.28), channel_id=1, source_target_pairs={{0,8},{4,28},{8,0},{12,20},{16,24},{20,12},{24,16},{28,4},{1,9},{5... | collective-permute-start | bytes 147464 | tf_op jit(solution)/shard_map/ppermute | solution.py:81
  21.3 1.1 %collective-permute-start.7 = (f32[48,128]{1,0:T(8,128)S(1)}, f32[48,128]{1,0:T(8,128)S(1)}, u32[]{:S(2)}, u32[]{:S(2)}) collective-permute-start(f32[48,128]{1,0:T(8,128)S(1)} %get-tuple-element.27), channel_id=1, source_target_pairs={{0,16},{4,20},{8,24},{12,28},{16,0},{20,4},{24,8},{28,12},{1,17},{... | collective-permute-start | bytes 73736 | tf_op jit(solution)/shard_map/ppermute | solution.py:81
  22.5 2.0 %collective-permute-done.8.pair.far = f32[96,128]{1,0:T(8,128)S(1)} collective-permute-done((f32[96,128]{1,0:T(8,128)S(1)}, f32[96,128]{1,0:T(8,128)S(1)}, u32[]{:S(2)}, u32[]{:S(2)}) %collective-permute-start.8) | collective-permute-done | bytes 49184 | tf_op jit(solution)/shard_map/ppermute | solution.py:81
  24.5 0.0 collective-permute-start.9
  24.5 0.0 copy-start
  24.5 1.6 %copy-done = f32[2,512,512]{2,1,0:T(8,128)S(1)} copy-done((f32[2,512,512]{2,1,0:T(8,128)S(1)}, f32[2,512,512]{2,1,0:T(8,128)}, u32[]{:S(2)}) %copy-start) | copy-done | bytes 2097176
  26.1 0.3 %shard_map.52 = (bf16[2,512,512]{2,1,0:T(8,128)(2,1)S(1)}, bf16[2,512,512]{2,1,0:T(8,128)(2,1)S(1)}) custom-call(f32[2,512,512]{2,1,0:T(8,128)S(1)} %copy-done), custom_call_target="tpu_custom_call" | custom-call | tf_op jit(solution)/shard_map/pallas_call | solution.py:271
  26.4 0.0 collective-permute-done.7.near
  26.4 0.0 collective-permute-done.9.handed
  26.4 1.2 %shard_map.53 = f32[3,16,512]{2,1,0:T(8,128)} custom-call(f32[48,128]{1,0:T(8,128)S(1)} %get-tuple-element.26.own, f32[48,128]{1,0:T(8,128)S(1)} %collective-permute-done.7.near, f32[96,128]{1,0:T(8,128)S(1)} %collective-permute-done.8.pair.far, f32[48,128]{1,0:T(8,128)S(1)} %collective-permute-done.9.handed, ...), custom_call_target="tpu_custom_call" | custom-call | tf_op jit(solution)/shard_map/pallas_call | solution.py:272
  (3 shorter events, 0.0 us)
Async XLA Ops:
  1.0 5.7 %collective-permute-start = (f32[112,128]{1,0:T(8,128)S(1)}, f32[112,128]{1,0:T(8,128)S(1)}, u32[]{:S(2)}, u32[]{:S(2)}) collective-permute-start(f32[112,128]{1,0:T(8,128)S(1)} %get-tuple-element.19), channel_id=1, source_target_pairs={{0,1},{1,0},{2,3},{3,2},{4,5},{5,4},{6,7},{7,6},{8,9},{9,8},{10,11... | collective-permute-start | bytes 172040 | tf_op jit(solution)/shard_map/ppermute | solution.py:81
  4.1 6.2 %collective-permute-start.1 = (f32[112,128]{1,0:T(8,128)S(1)}, f32[112,128]{1,0:T(8,128)S(1)}, u32[]{:S(2)}, u32[]{:S(2)}) collective-permute-start(f32[112,128]{1,0:T(8,128)S(1)} %get-tuple-element.20), channel_id=1, source_target_pairs={{0,2},{1,3},{2,0},{3,1},{4,6},{5,7},{6,4},{7,5},{8,10},{9,11},{10,... | collective-permute-start | bytes 172040 | tf_op jit(solution)/shard_map/ppermute | solution.py:81
  6.7 6.0 %collective-permute-start.2 = (f32[112,128]{1,0:T(8,128)S(1)}, f32[112,128]{1,0:T(8,128)S(1)}, u32[]{:S(2)}, u32[]{:S(2)}) collective-permute-start(f32[112,128]{1,0:T(8,128)S(1)} %get-tuple-element.21), channel_id=1, source_target_pairs={{0,3},{1,2},{2,1},{3,0},{4,7},{5,6},{6,5},{7,4},{8,11},{9,10},{10,... | collective-permute-start | bytes 172040 | tf_op jit(solution)/shard_map/ppermute | solution.py:81
  12.7 4.6 %collective-permute-start.6 = (f32[384,128]{1,0:T(8,128)S(1)}, f32[384,128]{1,0:T(8,128)S(1)}, u32[]{:S(2)}, u32[]{:S(2)}) collective-permute-start(f32[384,128]{1,0:T(8,128)S(1)} %get-tuple-element.23.own_ref), channel_id=1, source_target_pairs={{0,4},{4,0},{8,12},{12,8},{16,20},{20,16},{24,28},{28,24},{1,5},{5... | collective-permute-start | bytes 589832 | tf_op jit(solution)/shard_map/ppermute | solution.py:81
  12.8 1.5 %collective-permute-start.4 = (f32[16,512]{1,0:T(8,128)S(1)}, f32[16,512]{1,0:T(8,128)S(1)}, u32[]{:S(2)}, u32[]{:S(2)}) collective-permute-start(f32[16,512]{1,0:T(8,128)S(1)} %get-tuple-element.22.own.refs_0_), channel_id=1, source_target_pairs={{0,4},{4,0},{8,12},{12,8},{16,20},{20,16},{24,28},{28,24},{1,5},{5... | collective-permute-start | bytes 98312 | tf_op jit(solution)/shard_map/ppermute | solution.py:81
  14.3 5.8 %collective-permute-start.5 = (f32[32,512]{1,0:T(8,128)S(1)}, f32[32,512]{1,0:T(8,128)S(1)}, u32[]{:S(2)}, u32[]{:S(2)}) collective-permute-start(f32[32,512]{1,0:T(8,128)S(1)} %shard_map.48), channel_id=1, source_target_pairs={{0,8},{4,28},{8,0},{12,20},{16,24},{20,12},{24,16},{28,4},{1,9},{5... | collective-permute-start | bytes 196616 | tf_op jit(solution)/shard_map/ppermute | solution.py:81
  15.8 4.2 %collective-permute-start.3 = (f32[16,512]{1,0:T(8,128)S(1)}, f32[16,512]{1,0:T(8,128)S(1)}, u32[]{:S(2)}, u32[]{:S(2)}) collective-permute-start(f32[16,512]{1,0:T(8,128)S(1)} %get-tuple-element.22.own.refs_0_), channel_id=1, source_target_pairs={{0,16},{4,20},{8,24},{12,28},{16,0},{20,4},{24,8},{28,12},{1,17},{... | collective-permute-start | bytes 98312 | tf_op jit(solution)/shard_map/ppermute | solution.py:81
  17.3 0.7 %copy-start.1 = (s32[3,8]{1,0:T(4,128)S(1)}, s32[3,8]{1,0:T(4,128)}, u32[]{:S(2)}) copy-start(s32[3,8]{1,0:T(4,128)} %block_rows.1) | copy-start | bytes 292
  20.3 4.2 %collective-permute-start.8 = (f32[96,128]{1,0:T(8,128)S(1)}, f32[96,128]{1,0:T(8,128)S(1)}, u32[]{:S(2)}, u32[]{:S(2)}) collective-permute-start(f32[96,128]{1,0:T(8,128)S(1)} %get-tuple-element.28), channel_id=1, source_target_pairs={{0,8},{4,28},{8,0},{12,20},{16,24},{20,12},{24,16},{28,4},{1,9},{5... | collective-permute-start | bytes 147464 | tf_op jit(solution)/shard_map/ppermute | solution.py:81
  21.3 5.1 %collective-permute-start.7 = (f32[48,128]{1,0:T(8,128)S(1)}, f32[48,128]{1,0:T(8,128)S(1)}, u32[]{:S(2)}, u32[]{:S(2)}) collective-permute-start(f32[48,128]{1,0:T(8,128)S(1)} %get-tuple-element.27), channel_id=1, source_target_pairs={{0,16},{4,20},{8,24},{12,28},{16,0},{20,4},{24,8},{28,12},{1,17},{... | collective-permute-start | bytes 73736 | tf_op jit(solution)/shard_map/ppermute | solution.py:81
  24.5 1.9 %collective-permute-start.9 = (f32[48,128]{1,0:T(8,128)S(1)}, f32[48,128]{1,0:T(8,128)S(1)}, u32[]{:S(2)}, u32[]{:S(2)}) collective-permute-start(f32[48,128]{1,0:T(8,128)S(1)} %shard_map.51), channel_id=1, source_target_pairs={{0,4},{4,0},{8,12},{12,8},{16,20},{20,16},{24,28},{28,24},{1,5},{5... | collective-permute-start | bytes 73736 | tf_op jit(solution)/shard_map/ppermute | solution.py:81
  24.5 1.6 %copy-start = (f32[2,512,512]{2,1,0:T(8,128)S(1)}, f32[2,512,512]{2,1,0:T(8,128)}, u32[]{:S(2)}) copy-start(f32[2,512,512]{2,1,0:T(8,128)} %couplings.1) | copy-start | bytes 6291460

commit v4 on v3

--- a/solution.py
+++ b/solution.py
@@ -117,10 +117,20 @@
     out[pl.ds(pl.multiple_of((CORES - 1 - core) * rows, rows), rows), :] = other[...]
 
 
+def chains(sections):
+    return [(first, last) for last in range(1, sections) for first in reversed(range(last))]
+
+
 def couplings_kernel(couplings, high_ref, low_ref):
-    high, low = split(couplings[...])
-    high_ref[...] = high
-    low_ref[...] = low
+    order = chains(couplings.shape[0] + 1)
+    for at, (first, last) in enumerate(order):
+        if first == last - 1:
+            value = couplings[first]
+        else:
+            stacked = jnp.concatenate(split(couplings[first]), axis=0)
+            after = order.index((first + 1, last))
+            value = product(stacked, high_ref[after], low_ref[after])
+        high_ref[at], low_ref[at] = split(value)
 
 
 def place_kernel(fold, blocks_here, listed_here, block_size, block_rows, own_ref, other_ref, high_ref, low_ref):
@@ -188,34 +198,52 @@
     out[...] = pair[pl.ds(pl.multiple_of((CORES - 1 - core) * size, size), size), :]
 
 
-def finish_kernel(own, near, far, handed, high_ref, low_ref, out):
+def chained(values, high_ref, low_ref, blocks):
+    def rows(ref, at):
+        return jnp.concatenate([ref[at, block, :] for block in blocks], axis=0)
+
+    order = chains(len(values))
+    stacks = [jnp.concatenate(split(value), axis=0) for value in values]
+    totals = []
+    for last in range(len(values)):
+        total = None
+        for first in range(last):
+            at = order.index((first, last))
+            term = product(stacks[first], rows(high_ref, at), rows(low_ref, at))
+            term = term if (last - first) % 2 else -term
+            total = term if total is None else total + term
+        totals.append(total)
+    return totals
+
+
+def blocks_of(*distances):
+    chip = lax.div(lax.axis_index("row"), CORES)
+    return [pl.ds(pl.multiple_of((chip ^ away) * LANES, LANES), LANES) for away in distances]
+
+
+def advance(start, parts, blocks, high_ref, low_ref, out):
     sections, rows, _ = out.shape
-    chip = lax.div(lax.axis_index("row"), CORES)
-    core = lax.rem(lax.axis_index("row"), CORES)
-    size = sections * rows
-    previous = None
-    for section in range(sections):
-        at = section * rows
-        kept = far[pl.ds(pl.multiple_of(core * size + at, rows), rows), :]
-        given = handed[at : at + rows, :]
-        tiles = [
-            own[at : at + rows, :],
-            jnp.where(core == 0, kept, given),
-            near[at : at + rows, :],
-            jnp.where(core == 0, given, kept),
-        ]
-        step = 1
-        while step < len(tiles):
-            tiles = [
-                jnp.where((chip & step) != 0, tiles[i ^ step], tile) for i, tile in enumerate(tiles)
-            ]
-            step *= 2
-        value = jnp.concatenate(tiles, axis=1)
-        if previous is not None:
-            stacked = jnp.concatenate(split(previous), axis=0)
-            value = value + product(stacked, high_ref[section - 1], low_ref[section - 1])
-        previous = -value
-        out[section] = previous
+    values = [
+        [part[section * rows : (section + 1) * rows, :] for part in parts] for section in range(sections)
+    ]
+    totals = chained([jnp.concatenate(value, axis=1) for value in values], high_ref, low_ref, blocks)
+    for section, total in enumerate(totals):
+        base = jnp.zeros(out.shape[1:], jnp.float32) if start is None else start[section]
+        out[section] = base if total is None else base + total
+        for block, value in zip(blocks, values[section]):
+            out[section, :, block] = out[section, :, block] - value
+
+
+def partial_kernel(own, far, high_ref, low_ref, out):
+    core = lax.rem(lax.axis_index("row"), CORES)
+    size = own.shape[0]
+    kept = far.at[pl.ds(pl.multiple_of(core * size, size), size), :]
+    advance(None, [own, kept], blocks_of(0, jnp.where(core == 0, 1, 3)), high_ref, low_ref, out)
+
+
+def finish_kernel(partial, near, handed, high_ref, low_ref, out):
+    core = lax.rem(lax.axis_index("row"), CORES)
+    advance(partial, [near, handed], blocks_of(2, jnp.where(core == 0, 3, 1)), high_ref, low_ref, out)
 
 
 def gathered(inverse_tiles, factor_panels, block_rows, couplings):
@@ -268,10 +296,12 @@
     handed = swap(
         call(other_kernel, jax.ShapeDtypeStruct((sections * rows, LANES), f32), [VMEM])(from_far), "row", pair
     )
-    halves = call(couplings_kernel, [jax.ShapeDtypeStruct(couplings.shape, bf16)] * 2, [VMEM])(couplings)
-    return call(
-        finish_kernel, jax.ShapeDtypeStruct((sections, rows, piece_rows * count), f32), [VMEM] * 6
-    )(own, from_near, from_far, handed, *halves)
+    halves = call(
+        couplings_kernel, [jax.ShapeDtypeStruct((len(chains(sections)),) + couplings.shape[1:], bf16)] * 2, [VMEM]
+    )(couplings)
+    result = jax.ShapeDtypeStruct((sections, rows, piece_rows * count), f32)
+    partial = call(partial_kernel, result, [VMEM] * 4)(own, from_far, *halves)
+    return call(finish_kernel, result, [VMEM] * 5)(partial, from_near, handed, *halves)
 
 
 def on_device(inverse_tiles, factor_panels, block_rows, couplings):

time: 27.8 us -> 29.3 us (1.054)
  Pallas kernels: 3.68 us -> 5.22 us
    pallas_call x2 -> x3, Pallas kernels: 1.47 us -> 3.01 us  [the longest x1 1.59 us: gathered(): call(couplings_kernel, [jax.ShapeDtypeStruct((len(chains(sections)),) + c...]
  transfers between devices with their start and end apart: 10 -> 10, of which waited for: 5 -> 5; matrix products, arithmetic and copies ran while one was open for 0% -> 0% of each run, Pallas kernels for 4% -> 10%
where the time goes in v4:
time: 29.3 us; the launch traced here: 29.1 us
  starting transfers between devices  11.5 us (39%)
  waiting for transfers between devices  10.1 us (34%)
  Pallas kernels  5.22 us (18%)
  local copies, waits for them, and re-layouts  2.27 us (8%)
    ppermute x10, starting transfers between devices, swap(): return lax.ppermute(value, axis, pairs)  11.5 us
    ppermute x10, waiting for transfers between devices, swap(): return lax.ppermute(value, axis, pairs)  10.1 us
    unnamed x4, local copies, waits for them, and re-layouts  2.27 us
    pallas_call x1, Pallas kernels, gathered(): call(couplings_kernel, [jax.ShapeDtypeStruct((len(chains(sections)),) + c...  1.59 us
    pallas_call x1, Pallas kernels, gathered(): call(finish_kernel, result, [VMEM] * 5)(partial, from_near, handed, *halves)  1.04 us
    pallas_call x1, Pallas kernels, gathered(): call(functools.partial(pack_kernel, rows, fold), [jax.ShapeDtypeStruct((d...  0.99 us
    pallas_call x1, Pallas kernels, gathered(): call(functools.partial(place_kernel, fold, LANES // block_size, listed //...  0.9 us
  transfers between devices with their start and end apart: 10, of which 5 were waited for; matrix products, arithmetic and copies ran while one was open for 0% of the time, Pallas kernels for 10%

profile of v4, /device:TPU:0, one launch (start us, length us, event | category | flops | bytes accessed | tf_op | source)
XLA Modules:
  0.0 29.1 jit_solution(6615164158760324771)
XLA Ops:
  0.0 1.0 %shard_map.46 = (f32[112,128]{1,0:T(8,128)S(1)}, f32[112,128]{1,0:T(8,128)S(1)}, f32[112,128]{1,0:T(8,128)S(1)}, f32[112,128]{1,0:T(8,128)S(1)}) custom-call(f32[64,128]{1,0:T(8,128)} %tile_hbm.1, f32[3,64,64]{2,1,0:T(8,128)} %panel_hbm.1), custom_call_target="tpu_custom_call" | custom-call | tf_op jit(solution)/shard_map/pallas_call | solution.py:264
  1.0 3.1 %collective-permute-start = (f32[112,128]{1,0:T(8,128)S(1)}, f32[112,128]{1,0:T(8,128)S(1)}, u32[]{:S(2)}, u32[]{:S(2)}) collective-permute-start(f32[112,128]{1,0:T(8,128)S(1)} %get-tuple-element.19), channel_id=1, source_target_pairs={{0,1},{1,0},{2,3},{3,2},{4,5},{5,4},{6,7},{7,6},{8,9},{9,8},{10,11... | collective-permute-start | bytes 172040 | tf_op jit(solution)/shard_map/ppermute | solution.py:81
  4.1 2.6 %collective-permute-start.1 = (f32[112,128]{1,0:T(8,128)S(1)}, f32[112,128]{1,0:T(8,128)S(1)}, u32[]{:S(2)}, u32[]{:S(2)}) collective-permute-start(f32[112,128]{1,0:T(8,128)S(1)} %get-tuple-element.20), channel_id=1, source_target_pairs={{0,2},{1,3},{2,0},{3,1},{4,6},{5,7},{6,4},{7,5},{8,10},{9,11},{10,... | collective-permute-start | bytes 172040 | tf_op jit(solution)/shard_map/ppermute | solution.py:81
  6.7 0.0 collective-permute-start.2
  6.7 0.0 collective-permute-done.refs_1_
  6.7 3.6 %collective-permute-done.1.refs_2_ = f32[112,128]{1,0:T(8,128)S(1)} collective-permute-done((f32[112,128]{1,0:T(8,128)S(1)}, f32[112,128]{1,0:T(8,128)S(1)}, u32[]{:S(2)}, u32[]{:S(2)}) %collective-permute-start.1) | collective-permute-done | bytes 57376 | tf_op jit(solution)/shard_map/ppermute | solution.py:81
  10.3 2.4 %collective-permute-done.2.refs_3_ = f32[112,128]{1,0:T(8,128)S(1)} collective-permute-done((f32[112,128]{1,0:T(8,128)S(1)}, f32[112,128]{1,0:T(8,128)S(1)}, u32[]{:S(2)}, u32[]{:S(2)}) %collective-permute-start.2) | collective-permute-done | bytes 57376 | tf_op jit(solution)/shard_map/ppermute | solution.py:81
  12.7 0.1 collective-permute-start.6
  12.8 0.5 %collective-permute-start.4 = (f32[16,512]{1,0:T(8,128)S(1)}, f32[16,512]{1,0:T(8,128)S(1)}, u32[]{:S(2)}, u32[]{:S(2)}) collective-permute-start(f32[16,512]{1,0:T(8,128)S(1)} %get-tuple-element.22.own.refs_0_), channel_id=1, source_target_pairs={{0,4},{4,0},{8,12},{12,8},{16,20},{20,16},{24,28},{28,24},{1,5},{5... | collective-permute-start | bytes 98312 | tf_op jit(solution)/shard_map/ppermute | solution.py:81
  13.3 1.0 %collective-permute-done.4.other = f32[16,512]{1,0:T(8,128)S(1)} collective-permute-done((f32[16,512]{1,0:T(8,128)S(1)}, f32[16,512]{1,0:T(8,128)S(1)}, u32[]{:S(2)}, u32[]{:S(2)}) %collective-permute-start.4) | collective-permute-done | bytes 32800 | tf_op jit(solution)/shard_map/ppermute | solution.py:81
  14.3 1.6 %collective-permute-start.5 = (f32[32,512]{1,0:T(8,128)S(1)}, f32[32,512]{1,0:T(8,128)S(1)}, u32[]{:S(2)}, u32[]{:S(2)}) collective-permute-start(f32[32,512]{1,0:T(8,128)S(1)} %shard_map.48), channel_id=1, source_target_pairs={{0,8},{4,28},{8,0},{12,20},{16,24},{20,12},{24,16},{28,4},{1,9},{5... | collective-permute-start | bytes 196616 | tf_op jit(solution)/shard_map/ppermute | solution.py:81
  15.8 1.5 %collective-permute-start.3 = (f32[16,512]{1,0:T(8,128)S(1)}, f32[16,512]{1,0:T(8,128)S(1)}, u32[]{:S(2)}, u32[]{:S(2)}) collective-permute-start(f32[16,512]{1,0:T(8,128)S(1)} %get-tuple-element.22.own.refs_0_), channel_id=1, source_target_pairs={{0,16},{4,20},{8,24},{12,28},{16,0},{20,4},{24,8},{28,12},{1,17},{... | collective-permute-start | bytes 98312 | tf_op jit(solution)/shard_map/ppermute | solution.py:81
  17.3 0.0 collective-permute-done.6.other_ref
  17.3 0.0 copy-start.1
  17.3 0.7 %copy-done.1 = s32[3,8]{1,0:T(4,128)S(1)} copy-done((s32[3,8]{1,0:T(4,128)S(1)}, s32[3,8]{1,0:T(4,128)}, u32[]{:S(2)}) %copy-start.1) | copy-done | bytes 120
  18.0 0.9 %shard_map.49 = (bf16[512,384]{1,0:T(8,128)(2,1)S(1)}, bf16[512,384]{1,0:T(8,128)(2,1)S(1)}) custom-call(s32[3,8]{1,0:T(4,128)S(1)} %copy-done.1, f32[384,128]{1,0:T(8,128)S(1)} %get-tuple-element.23.own_ref, f32[384,128]{1,0:T(8,128)S(1)} %collective-permute-done.6.other_ref), custom_call_target="tpu_custom_call" | custom-call | tf_op jit(solution)/shard_map/pallas_call | solution.py:284
  18.9 1.1 %collective-permute-done.3.refs_1_ = f32[16,512]{1,0:T(8,128)S(1)} collective-permute-done((f32[16,512]{1,0:T(8,128)S(1)}, f32[16,512]{1,0:T(8,128)S(1)}, u32[]{:S(2)}, u32[]{:S(2)}) %collective-permute-start.3) | collective-permute-done | bytes 32800 | tf_op jit(solution)/shard_map/ppermute | solution.py:81
  20.0 0.0 collective-permute-done.5.refs_2_
  20.0 0.3 %shard_map.50 = (f32[48,128]{1,0:T(8,128)S(1)}, f32[48,128]{1,0:T(8,128)S(1)}, f32[96,128]{1,0:T(8,128)S(1)}) custom-call(f32[16,512]{1,0:T(8,128)S(1)} %get-tuple-element.22.own.refs_0_, f32[16,512]{1,0:T(8,128)S(1)} %collective-permute-done.3.refs_1_, f32[32,512]{1,0:T(8,128)S(1)} %collective-permute-done.5.refs_2_, ...), custom_call_target="tpu_custom_call" | custom-call | tf_op jit(solution)/shard_map/pallas_call | solution.py:289
  20.3 1.0 %collective-permute-start.7 = (f32[96,128]{1,0:T(8,128)S(1)}, f32[96,128]{1,0:T(8,128)S(1)}, u32[]{:S(2)}, u32[]{:S(2)}) collective-permute-start(f32[96,128]{1,0:T(8,128)S(1)} %get-tuple-element.27), channel_id=1, source_target_pairs={{0,8},{4,28},{8,0},{12,20},{16,24},{20,12},{24,16},{28,4},{1,9},{5... | collective-permute-start | bytes 147464 | tf_op jit(solution)/shard_map/ppermute | solution.py:81
  21.3 1.1 %collective-permute-start.8 = (f32[48,128]{1,0:T(8,128)S(1)}, f32[48,128]{1,0:T(8,128)S(1)}, u32[]{:S(2)}, u32[]{:S(2)}) collective-permute-start(f32[48,128]{1,0:T(8,128)S(1)} %get-tuple-element.30), channel_id=1, source_target_pairs={{0,16},{4,20},{8,24},{12,28},{16,0},{20,4},{24,8},{28,12},{1,17},{... | collective-permute-start | bytes 73736 | tf_op jit(solution)/shard_map/ppermute | solution.py:81
  22.5 2.0 %collective-permute-done.7.far.pair = f32[96,128]{1,0:T(8,128)S(1)} collective-permute-done((f32[96,128]{1,0:T(8,128)S(1)}, f32[96,128]{1,0:T(8,128)S(1)}, u32[]{:S(2)}, u32[]{:S(2)}) %collective-permute-start.7) | collective-permute-done | bytes 49184 | tf_op jit(solution)/shard_map/ppermute | solution.py:81
  24.5 0.0 collective-permute-start.9
  24.5 0.0 copy-start
  24.5 1.6 %copy-done = f32[2,512,512]{2,1,0:T(8,128)S(1)} copy-done((f32[2,512,512]{2,1,0:T(8,128)S(1)}, f32[2,512,512]{2,1,0:T(8,128)}, u32[]{:S(2)}) %copy-start) | copy-done | bytes 2097176
  26.1 1.6 %shard_map.51 = (bf16[3,512,512]{2,1,0:T(8,128)(2,1)S(1)}, bf16[3,512,512]{2,1,0:T(8,128)(2,1)S(1)}) custom-call(f32[2,512,512]{2,1,0:T(8,128)S(1)} %copy-done), custom_call_target="tpu_custom_call" | custom-call | tf_op jit(solution)/shard_map/pallas_call | solution.py:299
  27.7 0.4 %shard_map.52.partial = f32[3,16,512]{2,1,0:T(8,128)S(1)} custom-call(f32[48,128]{1,0:T(8,128)S(1)} %get-tuple-element.26.own, f32[96,128]{1,0:T(8,128)S(1)} %collective-permute-done.7.far.pair, bf16[3,512,512]{2,1,0:T(8,128)(2,1)S(1)} %get-tuple-element.28.high_ref, bf16[3,512,512]{2,1,0:T(8,128)(2,1)S(1)} %get-tuple-element.29.low_ref), custom_call_target="tpu_custom_call" | custom-call | tf_op jit(solution)/shard_map/pallas_call | solution.py:303
  28.1 0.0 collective-permute-done.8.near
  28.1 0.0 collective-permute-done.9.handed
  28.1 1.0 %shard_map.54 = f32[3,16,512]{2,1,0:T(8,128)} custom-call(f32[3,16,512]{2,1,0:T(8,128)S(1)} %shard_map.52.partial, f32[48,128]{1,0:T(8,128)S(1)} %collective-permute-done.8.near, f32[48,128]{1,0:T(8,128)S(1)} %collective-permute-done.9.handed, bf16[3,512,512]{2,1,0:T(8,128)(2,1)S(1)} %get-tuple-element.28.high_ref, ...), custom_call_target="tpu_custom_call" | custom-call | tf_op jit(solution)/shard_map/pallas_call | solution.py:304
  (3 shorter events, 0.0 us)
Async XLA Ops:
  1.0 5.7 %collective-permute-start = (f32[112,128]{1,0:T(8,128)S(1)}, f32[112,128]{1,0:T(8,128)S(1)}, u32[]{:S(2)}, u32[]{:S(2)}) collective-permute-start(f32[112,128]{1,0:T(8,128)S(1)} %get-tuple-element.19), channel_id=1, source_target_pairs={{0,1},{1,0},{2,3},{3,2},{4,5},{5,4},{6,7},{7,6},{8,9},{9,8},{10,11... | collective-permute-start | bytes 172040 | tf_op jit(solution)/shard_map/ppermute | solution.py:81
  4.1 6.2 %collective-permute-start.1 = (f32[112,128]{1,0:T(8,128)S(1)}, f32[112,128]{1,0:T(8,128)S(1)}, u32[]{:S(2)}, u32[]{:S(2)}) collective-permute-start(f32[112,128]{1,0:T(8,128)S(1)} %get-tuple-element.20), channel_id=1, source_target_pairs={{0,2},{1,3},{2,0},{3,1},{4,6},{5,7},{6,4},{7,5},{8,10},{9,11},{10,... | collective-permute-start | bytes 172040 | tf_op jit(solution)/shard_map/ppermute | solution.py:81
  6.7 6.0 %collective-permute-start.2 = (f32[112,128]{1,0:T(8,128)S(1)}, f32[112,128]{1,0:T(8,128)S(1)}, u32[]{:S(2)}, u32[]{:S(2)}) collective-permute-start(f32[112,128]{1,0:T(8,128)S(1)} %get-tuple-element.21), channel_id=1, source_target_pairs={{0,3},{1,2},{2,1},{3,0},{4,7},{5,6},{6,5},{7,4},{8,11},{9,10},{10,... | collective-permute-start | bytes 172040 | tf_op jit(solution)/shard_map/ppermute | solution.py:81
  12.7 4.6 %collective-permute-start.6 = (f32[384,128]{1,0:T(8,128)S(1)}, f32[384,128]{1,0:T(8,128)S(1)}, u32[]{:S(2)}, u32[]{:S(2)}) collective-permute-start(f32[384,128]{1,0:T(8,128)S(1)} %get-tuple-element.23.own_ref), channel_id=1, source_target_pairs={{0,4},{4,0},{8,12},{12,8},{16,20},{20,16},{24,28},{28,24},{1,5},{5... | collective-permute-start | bytes 589832 | tf_op jit(solution)/shard_map/ppermute | solution.py:81
  12.8 1.5 %collective-permute-start.4 = (f32[16,512]{1,0:T(8,128)S(1)}, f32[16,512]{1,0:T(8,128)S(1)}, u32[]{:S(2)}, u32[]{:S(2)}) collective-permute-start(f32[16,512]{1,0:T(8,128)S(1)} %get-tuple-element.22.own.refs_0_), channel_id=1, source_target_pairs={{0,4},{4,0},{8,12},{12,8},{16,20},{20,16},{24,28},{28,24},{1,5},{5... | collective-permute-start | bytes 98312 | tf_op jit(solution)/shard_map/ppermute | solution.py:81
  14.3 5.8 %collective-permute-start.5 = (f32[32,512]{1,0:T(8,128)S(1)}, f32[32,512]{1,0:T(8,128)S(1)}, u32[]{:S(2)}, u32[]{:S(2)}) collective-permute-start(f32[32,512]{1,0:T(8,128)S(1)} %shard_map.48), channel_id=1, source_target_pairs={{0,8},{4,28},{8,0},{12,20},{16,24},{20,12},{24,16},{28,4},{1,9},{5... | collective-permute-start | bytes 196616 | tf_op jit(solution)/shard_map/ppermute | solution.py:81
  15.8 4.2 %collective-permute-start.3 = (f32[16,512]{1,0:T(8,128)S(1)}, f32[16,512]{1,0:T(8,128)S(1)}, u32[]{:S(2)}, u32[]{:S(2)}) collective-permute-start(f32[16,512]{1,0:T(8,128)S(1)} %get-tuple-element.22.own.refs_0_), channel_id=1, source_target_pairs={{0,16},{4,20},{8,24},{12,28},{16,0},{20,4},{24,8},{28,12},{1,17},{... | collective-permute-start | bytes 98312 | tf_op jit(solution)/shard_map/ppermute | solution.py:81
  17.3 0.7 %copy-start.1 = (s32[3,8]{1,0:T(4,128)S(1)}, s32[3,8]{1,0:T(4,128)}, u32[]{:S(2)}) copy-start(s32[3,8]{1,0:T(4,128)} %block_rows.1) | copy-start | bytes 292
  20.3 4.2 %collective-permute-start.7 = (f32[96,128]{1,0:T(8,128)S(1)}, f32[96,128]{1,0:T(8,128)S(1)}, u32[]{:S(2)}, u32[]{:S(2)}) collective-permute-start(f32[96,128]{1,0:T(8,128)S(1)} %get-tuple-element.27), channel_id=1, source_target_pairs={{0,8},{4,28},{8,0},{12,20},{16,24},{20,12},{24,16},{28,4},{1,9},{5... | collective-permute-start | bytes 147464 | tf_op jit(solution)/shard_map/ppermute | solution.py:81
  21.3 6.8 %collective-permute-start.8 = (f32[48,128]{1,0:T(8,128)S(1)}, f32[48,128]{1,0:T(8,128)S(1)}, u32[]{:S(2)}, u32[]{:S(2)}) collective-permute-start(f32[48,128]{1,0:T(8,128)S(1)} %get-tuple-element.30), channel_id=1, source_target_pairs={{0,16},{4,20},{8,24},{12,28},{16,0},{20,4},{24,8},{28,12},{1,17},{... | collective-permute-start | bytes 73736 | tf_op jit(solution)/shard_map/ppermute | solution.py:81
  24.5 3.6 %collective-permute-start.9 = (f32[48,128]{1,0:T(8,128)S(1)}, f32[48,128]{1,0:T(8,128)S(1)}, u32[]{:S(2)}, u32[]{:S(2)}) collective-permute-start(f32[48,128]{1,0:T(8,128)S(1)} %shard_map.53), channel_id=1, source_target_pairs={{0,4},{4,0},{8,12},{12,8},{16,20},{20,16},{24,28},{28,24},{1,5},{5... | collective-permute-start | bytes 73736 | tf_op jit(solution)/shard_map/ppermute | solution.py:81
  24.5 1.6 %copy-start = (f32[2,512,512]{2,1,0:T(8,128)S(1)}, f32[2,512,512]{2,1,0:T(8,128)}, u32[]{:S(2)}) copy-start(f32[2,512,512]{2,1,0:T(8,128)} %couplings.1) | copy-start | bytes 6291460

commit v5 on v4

--- a/solution.py
+++ b/solution.py
@@ -81,6 +81,11 @@
     return lax.ppermute(value, axis, pairs)
 
 
+def shift(value, axis, distance):
+    count = lax.axis_size(axis)
+    return lax.ppermute(value, axis, [(i, (i + distance) % count) for i in range(count)])
+
+
 def pack_kernel(rows, fold, tile_hbm, panel_hbm, *refs):
     *outs, tile, panel, tile_done, panel_done = refs
     column = lax.axis_index("col")
@@ -91,7 +96,7 @@
     high = panel.shape[1] // fold
     tile_copy.wait()
     for away, out in enumerate(outs):
-        start = pl.multiple_of((column ^ away) * rows, rows)
+        start = pl.multiple_of(lax.rem(column + away, len(outs)) * rows, rows)
         out[panel.shape[0] * high :, :] = tile[pl.ds(start, rows), :]
     panel_copy.wait()
     for section in range(panel.shape[0]):
@@ -158,8 +163,9 @@
             high, low = split(jnp.concatenate(pieces, axis=0).T)
             for place in range(fold):
                 for block in range(listed_here):
-                    row = block_rows[section, (column ^ (first + place)) * listed_here + block]
-                    tile = (row // blocks_here) ^ column
+                    source = lax.rem(column + cols - (first + place), cols)
+                    row = block_rows[section, source * listed_here + block]
+                    tile = lax.rem(column + cols - row // blocks_here, cols)
                     start = tile * LANES + (row % blocks_here) * block_size
                     target = pl.ds(pl.multiple_of(start, block_size), block_size)
                     at = place * width + block * block_size
@@ -272,7 +278,7 @@
             pltpu.SemaphoreType.DMA,
         ],
     )(*[pltpu.with_memory_space_constraint(x, pltpu.HBM) for x in (inverse_tiles, factor_panels)])
-    arrived = [packed[0]] + [swap(packed[away], "col", [away]) for away in range(1, cols)]
+    arrived = [packed[0]] + [shift(packed[away], "col", away) for away in range(1, cols)]
     inverse, line = call(
         join_kernel,
         [jax.ShapeDtypeStruct((rows, order), f32), jax.ShapeDtypeStruct((cols * depth, LANES), f32)],

time: 29.3 us -> 27.8 us (0.949)
  waiting for transfers between devices: 10.1 us -> 7.11 us
  starting transfers between devices: 11.5 us -> 12.9 us
    ppermute x0 -> x3, starting transfers between devices: none -> 7.04 us  [shift(): lax.ppermute(value, axis, [(i, (i + distance) % count) for i in range(cou...]
    ppermute x10 -> x7, waiting for transfers between devices: 10.1 us -> 4.06 us  [swap(): return lax.ppermute(value, axis, pairs)]
    ppermute x10 -> x7, starting transfers between devices: 11.5 us -> 5.82 us  [swap(): return lax.ppermute(value, axis, pairs)]
    ppermute x0 -> x3, waiting for transfers between devices: none -> 3.05 us  [shift(): lax.ppermute(value, axis, [(i, (i + distance) % count) for i in range(cou...]
  transfers between devices with their start and end apart: 10 -> 10, of which waited for: 5 -> 6; matrix products, arithmetic and copies ran while one was open for 0% -> 0% of each run, Pallas kernels for 10% -> 11%
where the time goes in v5:
time: 27.8 us; the launch traced here: 27.6 us
  starting transfers between devices  12.9 us (46%)
  waiting for transfers between devices  7.11 us (26%)
  Pallas kernels  5.25 us (19%)
  local copies, waits for them, and re-layouts  2.27 us (8%)
    ppermute x3, starting transfers between devices, shift(): lax.ppermute(value, axis, [(i, (i + distance) % count) for i in range(cou...  7.04 us
    ppermute x7, starting transfers between devices, swap(): return lax.ppermute(value, axis, pairs)  5.82 us
    ppermute x7, waiting for transfers between devices, swap(): return lax.ppermute(value, axis, pairs)  4.06 us
    ppermute x3, waiting for transfers between devices, shift(): lax.ppermute(value, axis, [(i, (i + distance) % count) for i in range(cou...  3.05 us
    unnamed x4, local copies, waits for them, and re-layouts  2.27 us
    pallas_call x1, Pallas kernels, gathered(): call(couplings_kernel, [jax.ShapeDtypeStruct((len(chains(sections)),) + c...  1.59 us
    pallas_call x1, Pallas kernels, gathered(): call(finish_kernel, result, [VMEM] * 5)(partial, from_near, handed, *halves)  1.04 us
    pallas_call x1, Pallas kernels, gathered(): call(functools.partial(pack_kernel, rows, fold), [jax.ShapeDtypeStruct((d...  0.99 us
  transfers between devices with their start and end apart: 10, of which 6 were waited for; matrix products, arithmetic and copies ran while one was open for 0% of the time, Pallas kernels for 11%

profile of v5, /device:TPU:0, one launch (start us, length us, event | category | flops | bytes accessed | tf_op | source)
XLA Modules:
  0.0 27.6 jit_solution(69143621590242998)
XLA Ops:
  0.0 1.0 %shard_map.46 = (f32[112,128]{1,0:T(8,128)S(1)}, f32[112,128]{1,0:T(8,128)S(1)}, f32[112,128]{1,0:T(8,128)S(1)}, f32[112,128]{1,0:T(8,128)S(1)}) custom-call(f32[64,128]{1,0:T(8,128)} %tile_hbm.1, f32[3,64,64]{2,1,0:T(8,128)} %panel_hbm.1), custom_call_target="tpu_custom_call" | custom-call | tf_op jit(solution)/shard_map/pallas_call | solution.py:270
  1.0 3.1 %collective-permute-start = (f32[112,128]{1,0:T(8,128)S(1)}, f32[112,128]{1,0:T(8,128)S(1)}, u32[]{:S(2)}, u32[]{:S(2)}) collective-permute-start(f32[112,128]{1,0:T(8,128)S(1)} %get-tuple-element.19), channel_id=1, source_target_pairs={{0,1},{1,2},{2,3},{3,0},{4,5},{5,6},{6,7},{7,4},{8,9},{9,10},{10,1... | collective-permute-start | bytes 172040 | tf_op jit(solution)/shard_map/ppermute | solution.py:86
  4.1 2.6 %collective-permute-start.1 = (f32[112,128]{1,0:T(8,128)S(1)}, f32[112,128]{1,0:T(8,128)S(1)}, u32[]{:S(2)}, u32[]{:S(2)}) collective-permute-start(f32[112,128]{1,0:T(8,128)S(1)} %get-tuple-element.20), channel_id=1, source_target_pairs={{0,2},{1,3},{2,0},{3,1},{4,6},{5,7},{6,4},{7,5},{8,10},{9,11},{10,... | collective-permute-start | bytes 172040 | tf_op jit(solution)/shard_map/ppermute | solution.py:86
  6.7 1.3 %collective-permute-start.2 = (f32[112,128]{1,0:T(8,128)S(1)}, f32[112,128]{1,0:T(8,128)S(1)}, u32[]{:S(2)}, u32[]{:S(2)}) collective-permute-start(f32[112,128]{1,0:T(8,128)S(1)} %get-tuple-element.21), channel_id=1, source_target_pairs={{0,3},{1,0},{2,1},{3,2},{4,7},{5,4},{6,5},{7,6},{8,11},{9,8},{10,9... | collective-permute-start | bytes 172040 | tf_op jit(solution)/shard_map/ppermute | solution.py:86
  8.0 0.4 %collective-permute-done.refs_1_ = f32[112,128]{1,0:T(8,128)S(1)} collective-permute-done((f32[112,128]{1,0:T(8,128)S(1)}, f32[112,128]{1,0:T(8,128)S(1)}, u32[]{:S(2)}, u32[]{:S(2)}) %collective-permute-start) | collective-permute-done | bytes 57376 | tf_op jit(solution)/shard_map/ppermute | solution.py:86
  8.4 2.3 %collective-permute-done.1.refs_2_ = f32[112,128]{1,0:T(8,128)S(1)} collective-permute-done((f32[112,128]{1,0:T(8,128)S(1)}, f32[112,128]{1,0:T(8,128)S(1)}, u32[]{:S(2)}, u32[]{:S(2)}) %collective-permute-start.1) | collective-permute-done | bytes 57376 | tf_op jit(solution)/shard_map/ppermute | solution.py:86
  10.7 0.4 %collective-permute-done.2.refs_3_ = f32[112,128]{1,0:T(8,128)S(1)} collective-permute-done((f32[112,128]{1,0:T(8,128)S(1)}, f32[112,128]{1,0:T(8,128)S(1)}, u32[]{:S(2)}, u32[]{:S(2)}) %collective-permute-start.2) | collective-permute-done | bytes 57376 | tf_op jit(solution)/shard_map/ppermute | solution.py:86
  11.1 0.1 collective-permute-start.6
  11.2 0.5 %collective-permute-start.4 = (f32[16,512]{1,0:T(8,128)S(1)}, f32[16,512]{1,0:T(8,128)S(1)}, u32[]{:S(2)}, u32[]{:S(2)}) collective-permute-start(f32[16,512]{1,0:T(8,128)S(1)} %get-tuple-element.22.own.refs_0_), channel_id=1, source_target_pairs={{0,4},{4,0},{8,12},{12,8},{16,20},{20,16},{24,28},{28,24},{1,5},{5... | collective-permute-start | bytes 98312 | tf_op jit(solution)/shard_map/ppermute | solution.py:81
  11.7 1.0 %collective-permute-done.4.other = f32[16,512]{1,0:T(8,128)S(1)} collective-permute-done((f32[16,512]{1,0:T(8,128)S(1)}, f32[16,512]{1,0:T(8,128)S(1)}, u32[]{:S(2)}, u32[]{:S(2)}) %collective-permute-start.4) | collective-permute-done | bytes 32800 | tf_op jit(solution)/shard_map/ppermute | solution.py:81
  12.7 1.6 %collective-permute-start.5 = (f32[32,512]{1,0:T(8,128)S(1)}, f32[32,512]{1,0:T(8,128)S(1)}, u32[]{:S(2)}, u32[]{:S(2)}) collective-permute-start(f32[32,512]{1,0:T(8,128)S(1)} %shard_map.48), channel_id=1, source_target_pairs={{0,8},{4,28},{8,0},{12,20},{16,24},{20,12},{24,16},{28,4},{1,9},{5... | collective-permute-start | bytes 196616 | tf_op jit(solution)/shard_map/ppermute | solution.py:81
  14.3 1.5 %collective-permute-start.3 = (f32[16,512]{1,0:T(8,128)S(1)}, f32[16,512]{1,0:T(8,128)S(1)}, u32[]{:S(2)}, u32[]{:S(2)}) collective-permute-start(f32[16,512]{1,0:T(8,128)S(1)} %get-tuple-element.22.own.refs_0_), channel_id=1, source_target_pairs={{0,16},{4,20},{8,24},{12,28},{16,0},{20,4},{24,8},{28,12},{1,17},{... | collective-permute-start | bytes 98312 | tf_op jit(solution)/shard_map/ppermute | solution.py:81
  15.8 0.0 collective-permute-done.6.other_ref
  15.8 0.0 copy-start.1
  15.8 0.7 %copy-done.1 = s32[3,8]{1,0:T(4,128)S(1)} copy-done((s32[3,8]{1,0:T(4,128)S(1)}, s32[3,8]{1,0:T(4,128)}, u32[]{:S(2)}) %copy-start.1) | copy-done | bytes 120
  16.5 0.9 %shard_map.49 = (bf16[512,384]{1,0:T(8,128)(2,1)S(1)}, bf16[512,384]{1,0:T(8,128)(2,1)S(1)}) custom-call(s32[3,8]{1,0:T(4,128)S(1)} %copy-done.1, f32[384,128]{1,0:T(8,128)S(1)} %get-tuple-element.23.own_ref, f32[384,128]{1,0:T(8,128)S(1)} %collective-permute-done.6.other_ref), custom_call_target="tpu_custom_call" | custom-call | tf_op jit(solution)/shard_map/pallas_call | solution.py:290
  17.4 1.1 %collective-permute-done.3.refs_1_ = f32[16,512]{1,0:T(8,128)S(1)} collective-permute-done((f32[16,512]{1,0:T(8,128)S(1)}, f32[16,512]{1,0:T(8,128)S(1)}, u32[]{:S(2)}, u32[]{:S(2)}) %collective-permute-start.3) | collective-permute-done | bytes 32800 | tf_op jit(solution)/shard_map/ppermute | solution.py:81
  18.5 0.0 collective-permute-done.5.refs_2_
  18.5 0.3 %shard_map.50 = (f32[48,128]{1,0:T(8,128)S(1)}, f32[48,128]{1,0:T(8,128)S(1)}, f32[96,128]{1,0:T(8,128)S(1)}) custom-call(f32[16,512]{1,0:T(8,128)S(1)} %get-tuple-element.22.own.refs_0_, f32[16,512]{1,0:T(8,128)S(1)} %collective-permute-done.3.refs_1_, f32[32,512]{1,0:T(8,128)S(1)} %collective-permute-done.5.refs_2_, ...), custom_call_target="tpu_custom_call" | custom-call | tf_op jit(solution)/shard_map/pallas_call | solution.py:295
  18.8 1.0 %collective-permute-start.7 = (f32[96,128]{1,0:T(8,128)S(1)}, f32[96,128]{1,0:T(8,128)S(1)}, u32[]{:S(2)}, u32[]{:S(2)}) collective-permute-start(f32[96,128]{1,0:T(8,128)S(1)} %get-tuple-element.27), channel_id=1, source_target_pairs={{0,8},{4,28},{8,0},{12,20},{16,24},{20,12},{24,16},{28,4},{1,9},{5... | collective-permute-start | bytes 147464 | tf_op jit(solution)/shard_map/ppermute | solution.py:81
  19.8 1.2 %collective-permute-start.8 = (f32[48,128]{1,0:T(8,128)S(1)}, f32[48,128]{1,0:T(8,128)S(1)}, u32[]{:S(2)}, u32[]{:S(2)}) collective-permute-start(f32[48,128]{1,0:T(8,128)S(1)} %get-tuple-element.30), channel_id=1, source_target_pairs={{0,16},{4,20},{8,24},{12,28},{16,0},{20,4},{24,8},{28,12},{1,17},{... | collective-permute-start | bytes 73736 | tf_op jit(solution)/shard_map/ppermute | solution.py:81
  20.9 2.0 %collective-permute-done.7.far.pair = f32[96,128]{1,0:T(8,128)S(1)} collective-permute-done((f32[96,128]{1,0:T(8,128)S(1)}, f32[96,128]{1,0:T(8,128)S(1)}, u32[]{:S(2)}, u32[]{:S(2)}) %collective-permute-start.7) | collective-permute-done | bytes 49184 | tf_op jit(solution)/shard_map/ppermute | solution.py:81
  22.9 0.0 collective-permute-start.9
  22.9 0.0 copy-start
  22.9 1.6 %copy-done = f32[2,512,512]{2,1,0:T(8,128)S(1)} copy-done((f32[2,512,512]{2,1,0:T(8,128)S(1)}, f32[2,512,512]{2,1,0:T(8,128)}, u32[]{:S(2)}) %copy-start) | copy-done | bytes 2097176
  24.5 1.6 %shard_map.51 = (bf16[3,512,512]{2,1,0:T(8,128)(2,1)S(1)}, bf16[3,512,512]{2,1,0:T(8,128)(2,1)S(1)}) custom-call(f32[2,512,512]{2,1,0:T(8,128)S(1)} %copy-done), custom_call_target="tpu_custom_call" | custom-call | tf_op jit(solution)/shard_map/pallas_call | solution.py:305
  26.1 0.4 %shard_map.52.partial = f32[3,16,512]{2,1,0:T(8,128)S(1)} custom-call(f32[48,128]{1,0:T(8,128)S(1)} %get-tuple-element.26.own, f32[96,128]{1,0:T(8,128)S(1)} %collective-permute-done.7.far.pair, bf16[3,512,512]{2,1,0:T(8,128)(2,1)S(1)} %get-tuple-element.28.high_ref, bf16[3,512,512]{2,1,0:T(8,128)(2,1)S(1)} %get-tuple-element.29.low_ref), custom_call_target="tpu_custom_call" | custom-call | tf_op jit(solution)/shard_map/pallas_call | solution.py:309
  26.5 0.0 collective-permute-done.8.near
  26.5 0.0 collective-permute-done.9.handed
  26.5 1.0 %shard_map.54 = f32[3,16,512]{2,1,0:T(8,128)} custom-call(f32[3,16,512]{2,1,0:T(8,128)S(1)} %shard_map.52.partial, f32[48,128]{1,0:T(8,128)S(1)} %collective-permute-done.8.near, f32[48,128]{1,0:T(8,128)S(1)} %collective-permute-done.9.handed, bf16[3,512,512]{2,1,0:T(8,128)(2,1)S(1)} %get-tuple-element.28.high_ref, ...), custom_call_target="tpu_custom_call" | custom-call | tf_op jit(solution)/shard_map/pallas_call | solution.py:310
  (3 shorter events, 0.0 us)
Async XLA Ops:
  1.0 7.4 %collective-permute-start = (f32[112,128]{1,0:T(8,128)S(1)}, f32[112,128]{1,0:T(8,128)S(1)}, u32[]{:S(2)}, u32[]{:S(2)}) collective-permute-start(f32[112,128]{1,0:T(8,128)S(1)} %get-tuple-element.19), channel_id=1, source_target_pairs={{0,1},{1,2},{2,3},{3,0},{4,5},{5,6},{6,7},{7,4},{8,9},{9,10},{10,1... | collective-permute-start | bytes 172040 | tf_op jit(solution)/shard_map/ppermute | solution.py:86
  4.1 6.6 %collective-permute-start.1 = (f32[112,128]{1,0:T(8,128)S(1)}, f32[112,128]{1,0:T(8,128)S(1)}, u32[]{:S(2)}, u32[]{:S(2)}) collective-permute-start(f32[112,128]{1,0:T(8,128)S(1)} %get-tuple-element.20), channel_id=1, source_target_pairs={{0,2},{1,3},{2,0},{3,1},{4,6},{5,7},{6,4},{7,5},{8,10},{9,11},{10,... | collective-permute-start | bytes 172040 | tf_op jit(solution)/shard_map/ppermute | solution.py:86
  6.7 4.4 %collective-permute-start.2 = (f32[112,128]{1,0:T(8,128)S(1)}, f32[112,128]{1,0:T(8,128)S(1)}, u32[]{:S(2)}, u32[]{:S(2)}) collective-permute-start(f32[112,128]{1,0:T(8,128)S(1)} %get-tuple-element.21), channel_id=1, source_target_pairs={{0,3},{1,0},{2,1},{3,2},{4,7},{5,4},{6,5},{7,6},{8,11},{9,8},{10,9... | collective-permute-start | bytes 172040 | tf_op jit(solution)/shard_map/ppermute | solution.py:86
  11.1 4.7 %collective-permute-start.6 = (f32[384,128]{1,0:T(8,128)S(1)}, f32[384,128]{1,0:T(8,128)S(1)}, u32[]{:S(2)}, u32[]{:S(2)}) collective-permute-start(f32[384,128]{1,0:T(8,128)S(1)} %get-tuple-element.23.own_ref), channel_id=1, source_target_pairs={{0,4},{4,0},{8,12},{12,8},{16,20},{20,16},{24,28},{28,24},{1,5},{5... | collective-permute-start | bytes 589832 | tf_op jit(solution)/shard_map/ppermute | solution.py:81
  11.2 1.5 %collective-permute-start.4 = (f32[16,512]{1,0:T(8,128)S(1)}, f32[16,512]{1,0:T(8,128)S(1)}, u32[]{:S(2)}, u32[]{:S(2)}) collective-permute-start(f32[16,512]{1,0:T(8,128)S(1)} %get-tuple-element.22.own.refs_0_), channel_id=1, source_target_pairs={{0,4},{4,0},{8,12},{12,8},{16,20},{20,16},{24,28},{28,24},{1,5},{5... | collective-permute-start | bytes 98312 | tf_op jit(solution)/shard_map/ppermute | solution.py:81
  12.7 5.8 %collective-permute-start.5 = (f32[32,512]{1,0:T(8,128)S(1)}, f32[32,512]{1,0:T(8,128)S(1)}, u32[]{:S(2)}, u32[]{:S(2)}) collective-permute-start(f32[32,512]{1,0:T(8,128)S(1)} %shard_map.48), channel_id=1, source_target_pairs={{0,8},{4,28},{8,0},{12,20},{16,24},{20,12},{24,16},{28,4},{1,9},{5... | collective-permute-start | bytes 196616 | tf_op jit(solution)/shard_map/ppermute | solution.py:81
  14.3 4.2 %collective-permute-start.3 = (f32[16,512]{1,0:T(8,128)S(1)}, f32[16,512]{1,0:T(8,128)S(1)}, u32[]{:S(2)}, u32[]{:S(2)}) collective-permute-start(f32[16,512]{1,0:T(8,128)S(1)} %get-tuple-element.22.own.refs_0_), channel_id=1, source_target_pairs={{0,16},{4,20},{8,24},{12,28},{16,0},{20,4},{24,8},{28,12},{1,17},{... | collective-permute-start | bytes 98312 | tf_op jit(solution)/shard_map/ppermute | solution.py:81
  15.8 0.7 %copy-start.1 = (s32[3,8]{1,0:T(4,128)S(1)}, s32[3,8]{1,0:T(4,128)}, u32[]{:S(2)}) copy-start(s32[3,8]{1,0:T(4,128)} %block_rows.1) | copy-start | bytes 292
  18.8 4.2 %collective-permute-start.7 = (f32[96,128]{1,0:T(8,128)S(1)}, f32[96,128]{1,0:T(8,128)S(1)}, u32[]{:S(2)}, u32[]{:S(2)}) collective-permute-start(f32[96,128]{1,0:T(8,128)S(1)} %get-tuple-element.27), channel_id=1, source_target_pairs={{0,8},{4,28},{8,0},{12,20},{16,24},{20,12},{24,16},{28,4},{1,9},{5... | collective-permute-start | bytes 147464 | tf_op jit(solution)/shard_map/ppermute | solution.py:81
  19.8 6.8 %collective-permute-start.8 = (f32[48,128]{1,0:T(8,128)S(1)}, f32[48,128]{1,0:T(8,128)S(1)}, u32[]{:S(2)}, u32[]{:S(2)}) collective-permute-start(f32[48,128]{1,0:T(8,128)S(1)} %get-tuple-element.30), channel_id=1, source_target_pairs={{0,16},{4,20},{8,24},{12,28},{16,0},{20,4},{24,8},{28,12},{1,17},{... | collective-permute-start | bytes 73736 | tf_op jit(solution)/shard_map/ppermute | solution.py:81
  22.9 3.6 %collective-permute-start.9 = (f32[48,128]{1,0:T(8,128)S(1)}, f32[48,128]{1,0:T(8,128)S(1)}, u32[]{:S(2)}, u32[]{:S(2)}) collective-permute-start(f32[48,128]{1,0:T(8,128)S(1)} %shard_map.53), channel_id=1, source_target_pairs={{0,4},{4,0},{8,12},{12,8},{16,20},{20,16},{24,28},{28,24},{1,5},{5... | collective-permute-start | bytes 73736 | tf_op jit(solution)/shard_map/ppermute | solution.py:81
  22.9 1.6 %copy-start = (f32[2,512,512]{2,1,0:T(8,128)S(1)}, f32[2,512,512]{2,1,0:T(8,128)}, u32[]{:S(2)}) copy-start(f32[2,512,512]{2,1,0:T(8,128)} %couplings.1) | copy-start | bytes 6291460
